TPU v7x, 32 devices: a whole 2x2x4 slice. The times are simulated.
32 devices in a mesh: groups: 2 (over y), dom: 4 (over z), sub: 4 (over x, core).
Axes of the slice: x: 2, y: 2, z: 4, core: 2. Of those that a mesh axis runs over, the one named last changes fastest.
Arguments:
- positions: float32 [3, 16, 16, 128], P(None, ('groups', 'dom'), 'sub'), parts along dimension 1, may hold values from -50 to 80, as said below
- charge: float32 [16, 16, 128], P(('groups', 'dom'), 'sub'), parts along dimension 0, may hold values from -2.5 to 2.5
- radius: float32 [16, 16, 128], P(('groups', 'dom'), 'sub'), parts along dimension 0, may hold values from 1.3 to 2.2
- segment: int32 [16, 16, 128], P(('groups', 'dom'), 'sub'), parts along dimension 0, may hold values from 0 to 15, never falling along the last dimension, each value on 1 to 16 neighbouring positions
- near_tiles: int32 [16, 16, 8], P(('groups', 'dom'), 'sub'), parts along dimension 0, may hold values from 0 to 1, as said below
Outputs:
- born_radii: float32 [16, 16, 128], P(('groups', 'dom'), 'sub'), parts along dimension 0
- radius_grad: float32 [16, 16, 128], P(('groups', 'dom'), 'sub'), parts along dimension 0
- forces: float32 [3, 16, 16, 128], P(None, ('groups', 'dom'), 'sub'), parts along dimension 1
There are 2 independent parts, one for each index of `groups`. A program takes and returns all parts, laid end to end along the dimension named above; each array names one. Nothing has to cross between parts.
Inputs may be any that keep to these rules, and one draw needn't show every extreme that they name: `positions`: coordinates in angstroms; the third runs along the fiber. near_tiles[a, b, k] is 1 when the partner tile of step k is near tile (a, b), else 0. The relation is symmetric: a tile is near its partner exactly when the partner is near it by the opposite step. No tile is near a tile beyond either end of the first tile dimension; the second dimension closes around the fiber. `segment`: within each tile the component numbers never fall along the atoms, and each of the 16 components has 1 to 16 atoms.
All inputs are finite; a program needn't handle non-finite values.
Results may differ from a plain program's by a relative error of at most 0.0003.
Values sent between devices are 32-bit elements; how exact they have to be, the bound alone decides.
No kernel may reach another device: no remote copies, remote signals or barrier semaphores. Data moves between devices by JAX's collectives and lax.ppermute only.
A program may use at most 64 MiB of HBM per device.

v0:
```python
import jax
import jax.numpy as jnp
from jax import lax
from jax.sharding import PartitionSpec as P

CT = 16


neighbour_steps = ((-1, -1), (-1, 0), (-1, 1), (0, -1), (0, 1), (1, -1), (1, 0), (1, 1))
switch_span = 64.0
radius_factor = 1.5
highest = lax.Precision.HIGHEST
far_block = 1024


def passed_along(shard, axis, by):
    size = lax.axis_size(axis)
    return lax.ppermute(shard, axis, [(i, (i + by) % size) for i in range(size)])


def extended(cells, sides, width):
    for axis, dim in sides:
        count = lax.axis_size(axis)
        head = lax.slice_in_dim(cells, 0, width, axis=dim)
        tail = lax.slice_in_dim(cells, cells.shape[dim] - width, cells.shape[dim], axis=dim)
        cells = jnp.concatenate(
            [
                lax.ppermute(tail, axis, [(i, (i + 1) % count) for i in range(count)]),
                cells,
                lax.ppermute(head, axis, [((i + 1) % count, i) for i in range(count)]),
            ],
            axis=dim,
        )
    return cells


def far_keep(tile_along, tile_round, tile_near, comp_along, comp_round, around_count):
    struck = (tile_along[:, None] == comp_along[None, :]) & (
        tile_round[:, None] == comp_round[None, :]
    )
    for slot_index, (step_z, step_s) in enumerate(neighbour_steps):
        flagged = (tile_near[:, slot_index] == 1)[:, None]
        same_along = (tile_along + step_z)[:, None] == comp_along[None, :]
        same_round = jnp.mod(tile_round + step_s, around_count)[:, None] == comp_round[None, :]
        struck = struck | flagged & same_along & same_round
    return jnp.logical_not(struck)


def pair_distance(own_pos, part_pos):
    dist_sq = jnp.zeros(own_pos.shape[1:] + (part_pos.shape[-1],), own_pos.dtype)
    for axis_slot in range(3):
        apart_axis = own_pos[axis_slot][..., :, None] - part_pos[axis_slot][..., None, :]
        dist_sq = dist_sq + apart_axis * apart_axis
    return dist_sq


def born_distance(dist_sq, product):
    return jnp.sqrt(dist_sq + product * jnp.exp(-dist_sq / (4.0 * product)))


def tile_screen(own_pos, part_pos, part_rho, keep_mask):
    dist_sq = pair_distance(own_pos, part_pos)
    radius_sq = part_rho[..., None, :] * part_rho[..., None, :]
    denom_sq = dist_sq + radius_sq
    pair_term = radius_sq * part_rho[..., None, :] / (denom_sq * denom_sq)
    return jnp.sum(jnp.where(keep_mask, pair_term, 0.0), axis=-1)


def tile_energy(own_pos, own_born, part_pos, part_q, part_born, keep_mask):
    dist_sq = pair_distance(own_pos, part_pos)
    product = own_born[..., :, None] * part_born[..., None, :]
    pair_term = part_q[..., None, :] / born_distance(dist_sq, product)
    return jnp.sum(jnp.where(keep_mask, pair_term, 0.0), axis=-1)


def centre_distance(flat_pos, centre):
    dist_sq = jnp.zeros((flat_pos.shape[1], centre.shape[1]), flat_pos.dtype)
    for axis_slot in range(3):
        apart_axis = flat_pos[axis_slot][:, None] - centre[axis_slot][None, :]
        dist_sq = dist_sq + apart_axis * apart_axis
    return dist_sq


def screen_block(flat_pos, centre, volume, comp_radius, keep):
    dist_sq = centre_distance(flat_pos, centre)
    weight = dist_sq / (dist_sq + switch_span)
    denom_sq = dist_sq + comp_radius * comp_radius
    return jnp.sum(jnp.where(keep, volume * weight / (denom_sq * denom_sq), 0.0), axis=1)


def potential_block(flat_pos, flat_born, centre, total_q, comp_radius, keep):
    dist_sq = centre_distance(flat_pos, centre)
    weight = dist_sq / (dist_sq + switch_span)
    product = flat_born[:, None] * comp_radius[None, :]
    return jnp.sum(jnp.where(keep, total_q * weight / born_distance(dist_sq, product), 0.0), axis=1)


def block_split(values, block_size):
    shaped = values.reshape(values.shape[:-1] + (values.shape[-1] // block_size, block_size))
    return jnp.moveaxis(shaped, -2, 0)


def far_screening(flat_pos, centre, volume, comp_radius, comp_along, comp_round, keep_fn):
    block_size = min(centre.shape[1], far_block)

    def accumulate(running, pieces):
        keep = keep_fn(pieces[3], pieces[4])
        return (running + screen_block(flat_pos, pieces[0], pieces[1], pieces[2], keep), None)

    inputs = (
        block_split(centre, block_size),
        block_split(volume, block_size),
        block_split(comp_radius, block_size),
        block_split(comp_along, block_size),
        block_split(comp_round, block_size),
    )
    return lax.scan(
        jax.checkpoint(accumulate), jnp.zeros((flat_pos.shape[1],), jnp.float32), inputs
    )[0]


def far_potential(
    flat_pos, flat_born, centre, total_q, comp_radius, comp_along, comp_round, keep_fn
):
    block_size = min(centre.shape[1], far_block)

    def accumulate(running, pieces):
        keep = keep_fn(pieces[3], pieces[4])
        return (
            running + potential_block(flat_pos, flat_born, pieces[0], pieces[1], pieces[2], keep),
            None,
        )

    inputs = (
        block_split(centre, block_size),
        block_split(total_q, block_size),
        block_split(comp_radius, block_size),
        block_split(comp_along, block_size),
        block_split(comp_round, block_size),
    )
    return lax.scan(
        jax.checkpoint(accumulate), jnp.zeros((flat_pos.shape[1],), jnp.float32), inputs
    )[0]


def components(positions, charge, radius, segment):
    onehot = (segment[..., None] == jnp.arange(CT, dtype=jnp.int32)).astype(jnp.float32)
    members = jnp.sum(onehot, axis=2)
    centre = jnp.einsum("kabl,ablc->kabc", positions, onehot, precision=highest) / members
    total_q = jnp.einsum("abl,ablc->abc", charge, onehot, precision=highest)
    volume = jnp.einsum("abl,ablc->abc", radius * radius * radius, onehot, precision=highest)
    comp_radius = (
        radius_factor * jnp.einsum("abl,ablc->abc", radius, onehot, precision=highest) / members
    )
    return (onehot, members, centre, total_q, volume, comp_radius)


def sub_pass(rim_piece, direction):
    return passed_along(rim_piece, "sub", direction)


def dom_pass(rim_piece, direction):
    return passed_along(rim_piece, "dom", direction)


def fold_rims(window_grad):
    tile_rows = window_grad.shape[1] - 2
    tile_cols = window_grad.shape[2] - 2
    inner_grid = window_grad[:, :, 1 : tile_cols + 1]
    inner_grid = inner_grid.at[:, :, tile_cols - 1].add(sub_pass(window_grad[:, :, 0], -1))
    inner_grid = inner_grid.at[:, :, 0].add(sub_pass(window_grad[:, :, tile_cols + 1], 1))
    own_grid = inner_grid[:, 1 : tile_rows + 1]
    own_grid = own_grid.at[:, tile_rows - 1].add(dom_pass(inner_grid[:, 0], -1))
    own_grid = own_grid.at[:, 0].add(dom_pass(inner_grid[:, tile_rows + 1], 1))
    return own_grid


def centre_spread(grad_table):
    partial_sums = lax.psum_scatter(grad_table, "dom", scatter_dimension=1, tiled=True)
    return lax.psum_scatter(partial_sums, "sub", scatter_dimension=1, tiled=True)


def local(positions, charge, radius, segment, near_tiles):
    tile_rows, tile_cols, tile_width = charge.shape
    sub_count = lax.axis_size("sub")
    around_count = tile_cols * sub_count
    self_keep = jnp.arange(tile_width)[:, None] != jnp.arange(tile_width)[None, :]
    atom_stack = jnp.concatenate([positions, charge[None], radius[None]], axis=0)
    window = extended(atom_stack, (("dom", 1), ("sub", 2)), 1)
    win_pos = window[0:3]
    win_q = window[3]
    win_rho = window[4]
    onehot, members, centre, total_q, volume, comp_radius = components(
        positions, charge, radius, segment
    )
    comp_table = jnp.concatenate(
        [
            centre.reshape(3, -1),
            total_q.reshape(1, -1),
            volume.reshape(1, -1),
            comp_radius.reshape(1, -1),
        ],
        axis=0,
    )
    sub_table = lax.all_gather(comp_table, "sub", axis=1, tiled=True)
    all_table = lax.all_gather(sub_table, "dom", axis=1, tiled=True)
    all_centre = all_table[0:3]
    all_charge = all_table[3]
    all_volume = all_table[4]
    all_radius = all_table[5]
    per_device = tile_rows * tile_cols * CT
    entry_index = jnp.arange(all_table.shape[1], dtype=jnp.int32)
    owner_device = entry_index // per_device
    local_entry = entry_index % per_device
    comp_along = owner_device // sub_count * tile_rows + local_entry // (tile_cols * CT)
    comp_round = owner_device % sub_count * tile_cols + local_entry // CT % tile_cols
    dom_index = lax.axis_index("dom")
    sub_index = lax.axis_index("sub")
    shape_three = (tile_rows, tile_cols, tile_width)
    along_grid = dom_index * tile_rows + jnp.arange(tile_rows, dtype=jnp.int32)[:, None, None]
    round_grid = sub_index * tile_cols + jnp.arange(tile_cols, dtype=jnp.int32)[None, :, None]
    tile_along = jnp.broadcast_to(along_grid, shape_three).reshape(-1)
    tile_round = jnp.broadcast_to(round_grid, shape_three).reshape(-1)
    tile_near = jnp.broadcast_to(near_tiles[:, :, None, :], shape_three + (8,)).reshape(-1, 8)

    def keep_fn(block_along, block_round):
        return far_keep(tile_along, tile_round, tile_near, block_along, block_round, around_count)

    def window_part(values, step_z, step_s):
        return values[
            ..., 1 + step_z : 1 + step_z + tile_rows, 1 + step_s : 1 + step_s + tile_cols, :
        ]

    def born_of(own_pos, near_pos, far_centre):
        screening = tile_screen(
            own_pos, window_part(near_pos, 0, 0), window_part(win_rho, 0, 0), self_keep
        )
        for slot_index, (step_z, step_s) in enumerate(neighbour_steps):
            keep_mask = (near_tiles[..., slot_index] == 1)[..., None, None]
            screening = screening + tile_screen(
                own_pos,
                window_part(near_pos, step_z, step_s),
                window_part(win_rho, step_z, step_s),
                keep_mask,
            )
        far_part = far_screening(
            own_pos.reshape(3, -1),
            far_centre,
            all_volume,
            all_radius,
            comp_along,
            comp_round,
            keep_fn,
        )
        screening = screening + far_part.reshape(screening.shape)
        return radius * (1.0 + radius * screening)

    born_radii, born_back = jax.vjp(born_of, positions, win_pos, all_centre)
    win_born = extended(born_radii, (("dom", 0), ("sub", 1)), 1)

    def energy_of(own_pos, own_born, near_pos, near_born, far_centre):
        potential = tile_energy(
            own_pos,
            own_born,
            window_part(near_pos, 0, 0),
            window_part(win_q, 0, 0),
            window_part(near_born, 0, 0),
            self_keep,
        )
        for slot_index, (step_z, step_s) in enumerate(neighbour_steps):
            keep_mask = (near_tiles[..., slot_index] == 1)[..., None, None]
            potential = potential + tile_energy(
                own_pos,
                own_born,
                window_part(near_pos, step_z, step_s),
                window_part(win_q, step_z, step_s),
                window_part(near_born, step_z, step_s),
                keep_mask,
            )
        far_part = far_potential(
            own_pos.reshape(3, -1),
            own_born.reshape(-1),
            far_centre,
            all_charge,
            all_radius,
            comp_along,
            comp_round,
            keep_fn,
        )
        potential = potential + far_part.reshape(potential.shape)
        return -0.5 * jnp.sum(charge * (charge / own_born + potential))

    energy_back = jax.vjp(energy_of, positions, born_radii, win_pos, win_born, all_centre)[1]
    grad_pos, grad_born, grad_window, grad_wborn, grad_centre = energy_back(
        jnp.ones((), jnp.float32)
    )
    radius_grad = grad_born + fold_rims(grad_wborn[None])[0]
    chain_pos, chain_window, chain_centre = born_back(radius_grad)
    own_centre = centre_spread(grad_centre + chain_centre)
    per_member = own_centre.reshape(centre.shape) / members
    centre_part = jnp.einsum("ablc,kabc->kabl", onehot, per_member, precision=highest)
    total_grad = grad_pos + chain_pos + fold_rims(grad_window + chain_window) + centre_part
    return (born_radii, radius_grad, -total_grad)


def solution(mesh):
    placed = (
        P(None, ("groups", "dom"), "sub", None),
        P(("groups", "dom"), "sub", None),
        P(("groups", "dom"), "sub", None),
        P(("groups", "dom"), "sub", None),
        P(("groups", "dom"), "sub", None),
    )
    return jax.shard_map(
        local,
        mesh=mesh,
        in_specs=placed,
        out_specs=(
            P(("groups", "dom"), "sub", None),
            P(("groups", "dom"), "sub", None),
            P(None, ("groups", "dom"), "sub", None),
        ),
        check_vma=False,
    )
```

profile of v0, /device:TPU:0, one launch (start us, length us, event | category | flops | bytes accessed | tf_op | source)
XLA Modules:
  0.0 267.3 jit_solution(454773463730050776)
XLA Ops:
  7.2 0.7 pad_maximum_fusion
  8.0 3.1 %collective-permute-start = (f32[5,1,4,128]{3,2,1,0:T(4,128)S(1)}, f32[5,1,4,128]{3,2,1,0:T(4,128)S(1)}, u32[]{:S(2)}, u32[]{:S(2)}) collective-permute-start(f32[5,1,4,128]{3,2,1,0:T(4,128)S(1)} %get-tuple-element.1764), channel_id=1, source_target_pairs={{0,4},{4,8},{8,12},{12,0},{1,5},{5,9},{9,13},{13,1},{2,6},{6,10},{... | collective-permute-start | bytes 30728 | tf_op jit(solution)/shard_map/ppermute | solution.py:28
  11.1 2.1 collective-permute-start.1
  13.2 0.7 broadcast_multiply_fusion
  14.0 0.8 convert_reduce_fusion
  14.8 0.9 fusion.465
  15.7 0.9 fusion.122
  16.7 0.7 multiply_multiply_fusion.31
  17.4 0.8 fusion.466
  18.3 0.9 fusion.467
  19.3 1.4 fusion.491
  20.8 5.2 %all_gather.6 = f32[6,512]{1,0:T(8,128)S(1)} all-gather(f32[6,128]{1,0:T(8,128)S(1)} %pad_maximum_fusion.40), channel_id=1, replica_groups=mesh['groups'=2,'dom'=4,'sub'=4] {'sub'}, dimensions={1}, use_global_device_ids=true | all-gather | bytes 15360 | tf_op jit(solution)/shard_map/all_gather | solution.py:205
  26.0 0.8 broadcast_in_dim.489
  26.8 13.1 %all_gather.7 = f32[6,2048]{1,0:T(8,128)S(1)} all-gather(f32[6,512]{1,0:T(8,128)S(1)} %all_gather.6), channel_id=1, replica_groups=mesh['groups'=2,'dom'=4,'sub'=4] {'dom'}, dimensions={1}, use_global_device_ids=true | all-gather | bytes 61440 | tf_op jit(solution)/shard_map/all_gather | solution.py:206
  40.0 0.7 reshape.1777
  40.8 0.8 pad_maximum_fusion.11
  41.7 1.7 collective-permute-start.3
  43.4 0.7 maximum_bitcast_fusion.17
  44.2 0.6 collective-permute-done.2
  44.9 20.9 %while.65 = (s32[]{:T(128)}, f32[1024]{0:T(1024)S(1)}, s32[2,1024]{1,0:T(2,128)S(1)}, s32[2,1024]{1,0:T(2,128)S(1)}, pred[1024,1]{0,1:T(4,128)(4,1)S(1)}, /*inde...) while((s32[]{:T(128)}, f32[1024]{0:T(1024)S(1)}, ...), condition=%wide.region_12.13_spmd.clone.clone.clone, body=%wide.region_10.12_spmd.clone.clone.clone.sunk | while | flops 50371588 | bytes 205115 | solution.py:117
  45.4 10.0 %select_reduce_fusion.11 = f32[1024]{0:T(1024)S(1)} fusion(f32[1024]{0:T(1024)S(1)} %bitcast.622, f32[1024]{0:T(1024)S(1)} %bitcast.592, f32[1024]{0:T(1024)S(1)} %bitcast.691, f32[1024]{0:T(1024)S(1)} %bitcast.591, f32[1024]{0:T(1024)S(1)} %bitcast.695, f32[1024]{0:T(1024)S(1)} %bitcast.590, f32[1024]{0:T(1024)S(1)} %bitcast.693, ...), kind=kLoop, calls=%fused_computation.229.clone.1 | loop fusion | flops 50330624 | bytes 81920 | tf_op jit(solution)/shard_map/jvp()/while/body/eval_jaxpr/reduce_sum | solution.py:88
  55.8 10.0 %select_reduce_fusion.11 = f32[1024]{0:T(1024)S(1)} fusion(f32[1024]{0:T(1024)S(1)} %bitcast.622, f32[1024]{0:T(1024)S(1)} %bitcast.592, f32[1024]{0:T(1024)S(1)} %bitcast.691, f32[1024]{0:T(1024)S(1)} %bitcast.591, f32[1024]{0:T(1024)S(1)} %bitcast.695, f32[1024]{0:T(1024)S(1)} %bitcast.590, f32[1024]{0:T(1024)S(1)} %bitcast.693, ...), kind=kLoop, calls=%fused_computation.229.clone.1 | loop fusion | flops 50330624 | bytes 81920 | tf_op jit(solution)/shard_map/jvp()/while/body/eval_jaxpr/reduce_sum | solution.py:88
  65.9 0.9 select_reduce_fusion.7
  66.8 0.9 select_reduce_fusion.4
  67.7 0.9 select_reduce_fusion.2
  68.6 1.3 select_reduce_fusion.8
  70.1 3.7 %collective-permute-start.5 = (f32[1,4,128]{2,1,0:T(4,128)S(1)}, f32[1,4,128]{2,1,0:T(4,128)S(1)}, u32[]{:S(2)}, u32[]{:S(2)}) collective-permute-start(f32[1,4,128]{2,1,0:T(4,128)S(1)} %get-tuple-element.1814), channel_id=1, source_target_pairs={{4,0},{8,4},{12,8},{0,12},{5,1},{9,5},{13,9},{1,13},{6,2},{10,6},{... | collective-permute-start | bytes 6152 | tf_op jit(solution)/shard_map/ppermute | solution.py:30
  73.8 61.9 %while.63 = (s32[]{:T(128)}, f32[3,1024]{1,0:T(4,128)S(1)}, f32[1024]{0:T(1024)S(1)}, f32[1024]{0:T(1024)S(1)}, f32[2,3,1024]{2,1,0:T(4,128)S(1)}, /*index=5*/f3...) while((s32[]{:T(128)}, f32[3,1024]{1,0:T(4,128)S(1)}, ...), condition=%wide.region_21.22_spmd.clone, body=%wide.region_13.21_spmd.clone.sunk | while | flops 160494592 | bytes 520676 | solution.py:141
  74.3 14.4 %multiply_reduce_fusion.20 = f32[1024]{0:T(1024)S(1)} fusion(f32[1024]{0:T(1024)S(1)} %bitcast.599, f32[1024]{0:T(1024)S(1)} %get-tuple-element.2180, f32[1024]{0:T(1024)S(1)} %bitcast.606, f32[1024]{0:T(1024)S(1)} %bitcast.615, f32[1024]{0:T(1024)S(1)} %bitcast.608, f32[1024]{0:T(1024)S(1)} %bitcast.617, f32[1024]{0:T(1024)S(1)} %bitcast.604, ...), kind=kLoop, calls=%fused_computation.76.clone.1 | loop fusion | flops 72350720 | bytes 90112 | tf_op jit(solution)/shard_map/transpose(jvp())/while/body/eval_jaxpr/checkpoint/reduce_sum | solution.py:94
  88.7 15.9 %fusion.521 = (f32[1024]{0:T(1024)S(1)}, f32[1024]{0:T(1024)S(1)}, f32[1024]{0:T(1024)S(1)}, f32[1024]{0:T(1024)S(1)}, f32[1024]{0:T(1024)S(1)}, /*index=5*/f32[1024]{0:T(1024)S(1)}) fusion(f32[1024]{0:T(1024)S(1)} %bitcast.605, f32[1024]{0:T(1024)S(1)} %bitcast.614, f32[1024]{0:T(1024)S(1)} %bitcast.609, f32[1024]{0:T(1024)S(1)} %bitcast.618, ...), kind=kLoop, calls=%fused_computation.89.clone.1 | loop fusion | flops 88074240 | bytes 110592 | tf_op jit(solution)/shard_map/transpose(jvp())/while/body/eval_jaxpr/checkpoint/reduce_sum | solution.py:79
  105.2 14.4 %multiply_reduce_fusion.20 = f32[1024]{0:T(1024)S(1)} fusion(f32[1024]{0:T(1024)S(1)} %bitcast.599, f32[1024]{0:T(1024)S(1)} %get-tuple-element.2180, f32[1024]{0:T(1024)S(1)} %bitcast.606, f32[1024]{0:T(1024)S(1)} %bitcast.615, f32[1024]{0:T(1024)S(1)} %bitcast.608, f32[1024]{0:T(1024)S(1)} %bitcast.617, f32[1024]{0:T(1024)S(1)} %bitcast.604, ...), kind=kLoop, calls=%fused_computation.76.clone.1 | loop fusion | flops 72350720 | bytes 90112 | tf_op jit(solution)/shard_map/transpose(jvp())/while/body/eval_jaxpr/checkpoint/reduce_sum | solution.py:94
  119.6 15.9 %fusion.521 = (f32[1024]{0:T(1024)S(1)}, f32[1024]{0:T(1024)S(1)}, f32[1024]{0:T(1024)S(1)}, f32[1024]{0:T(1024)S(1)}, f32[1024]{0:T(1024)S(1)}, /*index=5*/f32[1024]{0:T(1024)S(1)}) fusion(f32[1024]{0:T(1024)S(1)} %bitcast.605, f32[1024]{0:T(1024)S(1)} %bitcast.614, f32[1024]{0:T(1024)S(1)} %bitcast.609, f32[1024]{0:T(1024)S(1)} %bitcast.618, ...), kind=kLoop, calls=%fused_computation.89.clone.1 | loop fusion | flops 88074240 | bytes 110592 | tf_op jit(solution)/shard_map/transpose(jvp())/while/body/eval_jaxpr/checkpoint/reduce_sum | solution.py:79
  135.8 1.7 collective-permute-start.6
  137.5 1.3 collective-permute-done.7
  138.8 3.7 %fusion.382 = (f32[2,4,128]{2,1,0:T(4,128)S(1)}, f32[2,4,128]{2,1,0:T(4,128)S(1)}, f32[2,4,128]{2,1,0:T(4,128)S(1)}, f32[2,4,128]{2,1,0:T(4,128)S(1)}, f32[2,4,1...) fusion(f32[2,4,128]{2,1,0:T(4,128)S(1)} %get-tuple-element.1743, ...), kind=kLoop, calls=%fused_computation.648 | loop fusion | flops 13352960 | bytes 126992 | tf_op jit(solution)/shard_map/transpose(jvp())/reduce_sum | solution.py:52
  142.7 3.7 %fusion.406 = (f32[2,4,128]{2,1,0:T(4,128)S(1)}, f32[2,4,128]{2,1,0:T(4,128)S(1)}, f32[2,4,128]{2,1,0:T(4,128)S(1)}, f32[2,4,128]{2,1,0:T(4,128)S(1)}, f32[2,4,1...) fusion(f32[2,4,128]{2,1,0:T(4,128)S(1)} %get-tuple-element.1739, ...), kind=kLoop, calls=%fused_computation.672 | loop fusion | flops 13352960 | bytes 126992 | tf_op jit(solution)/shard_map/transpose(jvp())/reduce_sum | solution.py:52
  146.6 3.7 %fusion.430 = (f32[2,4,128]{2,1,0:T(4,128)S(1)}, f32[2,4,128]{2,1,0:T(4,128)S(1)}, f32[2,4,128]{2,1,0:T(4,128)S(1)}, f32[2,4,128]{2,1,0:T(4,128)S(1)}, f32[2,4,1...) fusion(f32[2,4,128]{2,1,0:T(4,128)S(1)} %get-tuple-element.1759, ...), kind=kLoop, calls=%fused_computation.696 | loop fusion | flops 13352960 | bytes 126992 | tf_op jit(solution)/shard_map/transpose(jvp())/reduce_sum | solution.py:52
  150.5 5.0 %fusion.358 = (f32[2,4,128]{2,1,0:T(4,128)S(1)}, f32[2,4,128]{2,1,0:T(4,128)S(1)}, f32[2,4,128]{2,1,0:T(4,128)S(1)}, f32[2,4,128]{2,1,0:T(4,128)S(1)}, f32[2,4,1...) fusion(f32[2,4,128]{2,1,0:T(4,128)S(1)} %get-tuple-element.1734, ...), kind=kLoop, calls=%fused_computation.624 | loop fusion | flops 20029440 | bytes 180240 | tf_op jit(solution)/shard_map/transpose(jvp())/reduce_sum | solution.py:52
  155.8 1.8 collective-permute-start.8
  157.9 1.0 collective-permute-done.8
  158.9 2.0 collective-permute-done.9
  160.9 0.2 collective-permute-start.10
  161.2 1.9 collective-permute-start.11
  163.1 1.5 collective-permute-done.10
  164.6 2.1 collective-permute-done.11
  166.7 0.6 multiply_multiply_fusion.30
  167.3 2.0 fusion.396
  169.3 2.0 fusion.372
  171.3 2.0 fusion.384
  173.3 2.8 %fusion.360 = (f32[2,4,128]{2,1,0:T(4,128)S(1)}, f32[2,4,128]{2,1,0:T(4,128)S(1)}, f32[2,4,128]{2,1,0:T(4,128)S(1)}, f32[2,4,128]{2,1,0:T(4,128)S(1)}, f32[2,4,1...) fusion(f32[2,4,128]{2,1,0:T(4,128)S(1)} %get-tuple-element.1734, ...), kind=kLoop, calls=%fused_computation.626 | loop fusion | flops 11778048 | bytes 155664 | tf_op jit(solution)/shard_map/transpose(jvp())/reduce_sum | solution.py:52
  177.1 0.5 collective-permute-start.13
  177.6 0.8 collective-permute-done.12
  178.4 1.8 collective-permute-done.13
  180.2 0.3 collective-permute-start.14
  180.6 28.3 %while.64 = (s32[]{:T(128)}, f32[3,1024]{1,0:T(4,128)S(1)}, f32[1024]{0:T(1024)S(1)}, f32[2,3,1024]{2,1,0:T(4,128)S(1)}, f32[2,3,1024]{2,1,0:T(4,128)S(1)}, /*in...) while((s32[]{:T(128)}, f32[3,1024]{1,0:T(4,128)S(1)}, ...), condition=%wide.region_74.75_spmd.clone, body=%wide.region_67.74_spmd.clone.sunk | while | flops 78705664 | bytes 426451 | solution.py:117
  181.1 13.6 %fusion.524 = (f32[1024]{0:T(1024)S(1)}, f32[1024]{0:T(1024)S(1)}, f32[1024]{0:T(1024)S(1)}, f32[1024]{0:T(1024)S(1)}, f32[1024]{0:T(1024)S(1)}, /*index=5*/f32[1024]{0:T(1024)S(1)}) fusion(f32[1024]{0:T(1024)S(1)} %bitcast.610, f32[1024]{0:T(1024)S(1)} %bitcast.619, f32[1024]{0:T(1024)S(1)} %bitcast.612, f32[1024]{0:T(1024)S(1)} %bitcast.621, ...), kind=kLoop, calls=%fused_computation.178.clone.1 | loop fusion | flops 78637056 | bytes 106496 | tf_op jit(solution)/shard_map/transpose(jvp())/while/body/eval_jaxpr/checkpoint/reduce_sum | solution.py:79
  195.2 13.6 %fusion.524 = (f32[1024]{0:T(1024)S(1)}, f32[1024]{0:T(1024)S(1)}, f32[1024]{0:T(1024)S(1)}, f32[1024]{0:T(1024)S(1)}, f32[1024]{0:T(1024)S(1)}, /*index=5*/f32[1024]{0:T(1024)S(1)}) fusion(f32[1024]{0:T(1024)S(1)} %bitcast.610, f32[1024]{0:T(1024)S(1)} %bitcast.619, f32[1024]{0:T(1024)S(1)} %bitcast.612, f32[1024]{0:T(1024)S(1)} %bitcast.621, ...), kind=kLoop, calls=%fused_computation.178.clone.1 | loop fusion | flops 78637056 | bytes 106496 | tf_op jit(solution)/shard_map/transpose(jvp())/while/body/eval_jaxpr/checkpoint/reduce_sum | solution.py:79
  208.9 1.4 copy.110
  210.4 2.0 collective-permute-start.15
  212.4 24.8 %reduce-scatter.7.cloned.1.call-done = f32[512,3]{1,0:T(8,128)} async-done(((f32[2048,3]{1,0:T(8,128)}), f32[512,3]{1,0:T(8,128)}) %reduce-scatter.7.cloned.1.call-update) | async-done | bytes 6160
  237.2 21.3 %reduce-scatter.9.cloned.1.call-done = f32[128,3]{1,0:T(8,128)} async-done(((f32[512,3]{1,0:T(8,128)}), f32[128,3]{1,0:T(8,128)}) %reduce-scatter.9.cloned.1.call-update) | async-done | bytes 1552
  258.5 1.0 copy.114
  259.5 0.3 add_negate_fusion
  259.8 0.6 copy.103
  (328 shorter events, 5.3 us)
Async XLA Ops:
  7.2 37.0 %copy-start = (f32[3,2,4,128]{3,2,1,0:T(4,128)S(1)}, f32[3,2,4,128]{3,2,1,0:T(4,128)}, u32[]{:S(2)}) copy-start(f32[3,2,4,128]{3,2,1,0:T(4,128)} %param.27) | copy-start | bytes 36868
  7.2 37.6 %copy-start.2 = (f32[2,4,128]{2,1,0:T(4,128)S(1)}, f32[2,4,128]{2,1,0:T(4,128)}, u32[]{:S(2)}) copy-start(f32[2,4,128]{2,1,0:T(4,128)} %param.29) | copy-start | bytes 12292
  7.2 37.6 %copy-start.3 = (f32[2,4,128]{2,1,0:T(4,128)S(1)}, f32[2,4,128]{2,1,0:T(4,128)}, u32[]{:S(2)}) copy-start(f32[2,4,128]{2,1,0:T(4,128)} %param.28) | copy-start | bytes 12292
  7.2 230.0 %reduce-scatter.7.cloned.1.call-start = ((), (), s32[]{:S(2)}) async-start(), calls=%async_computation.2 | async-start | bytes 1310720
  8.0 32.8 %collective-permute-start = (f32[5,1,4,128]{3,2,1,0:T(4,128)S(1)}, f32[5,1,4,128]{3,2,1,0:T(4,128)S(1)}, u32[]{:S(2)}, u32[]{:S(2)}) collective-permute-start(f32[5,1,4,128]{3,2,1,0:T(4,128)S(1)} %get-tuple-element.1764), channel_id=1, source_target_pairs={{0,4},{4,8},{8,12},{12,0},{1,5},{5,9},{9,13},{13,1},{2,6},{6,10},{... | collective-permute-start | bytes 30728 | tf_op jit(solution)/shard_map/ppermute | solution.py:28
  11.1 29.7 %collective-permute-start.1 = (f32[5,1,4,128]{3,2,1,0:T(4,128)S(1)}, f32[5,1,4,128]{3,2,1,0:T(4,128)S(1)}, u32[]{:S(2)}, u32[]{:S(2)}) collective-permute-start(f32[5,1,4,128]{3,2,1,0:T(4,128)S(1)} %get-tuple-element.1765), channel_id=1, source_target_pairs={{4,0},{8,4},{12,8},{0,12},{5,1},{9,5},{13,9},{1,13},{6,2},{10,6},{... | collective-permute-start | bytes 30728 | tf_op jit(solution)/shard_map/ppermute | solution.py:30
  41.6 3.1 %collective-permute-start.2 = (f32[5,4,1,128]{3,2,1,0:T(1,128)S(1)}, f32[5,4,1,128]{3,2,1,0:T(1,128)S(1)}, u32[]{:S(2)}, u32[]{:S(2)}) collective-permute-start(f32[5,4,1,128]{3,2,1,0:T(1,128)S(1)} %get-tuple-element.1746), channel_id=1, source_target_pairs={{0,1},{1,2},{2,3},{3,0},{4,5},{5,6},{6,7},{7,4},{8,9},{9,10},{10,1... | collective-permute-start | bytes 30728 | tf_op jit(solution)/shard_map/ppermute | solution.py:28
  41.7 24.1 %collective-permute-start.3 = (f32[5,4,1,128]{3,2,1,0:T(1,128)S(1)}, f32[5,4,1,128]{3,2,1,0:T(1,128)S(1)}, u32[]{:S(2)}, u32[]{:S(2)}) collective-permute-start(f32[5,4,1,128]{3,2,1,0:T(1,128)S(1)} %get-tuple-element.1747), channel_id=1, source_target_pairs={{1,0},{2,1},{3,2},{0,3},{5,4},{6,5},{7,6},{4,7},{9,8},{10,9},{11,1... | collective-permute-start | bytes 30728 | tf_op jit(solution)/shard_map/ppermute | solution.py:30
  44.9 28.9 %copy-start.1 = (s32[2,4,8]{2,1,0:T(4,128)S(1)}, s32[2,4,8]{2,1,0:T(4,128)}, u32[]{:S(2)}) copy-start(s32[2,4,8]{2,1,0:T(4,128)} %param.31) | copy-start | bytes 772
  69.9 65.8 %collective-permute-start.4 = (f32[1,4,128]{2,1,0:T(4,128)S(1)}, f32[1,4,128]{2,1,0:T(4,128)S(1)}, u32[]{:S(2)}, u32[]{:S(2)}) collective-permute-start(f32[1,4,128]{2,1,0:T(4,128)S(1)} %get-tuple-element.1813), channel_id=1, source_target_pairs={{0,4},{4,8},{8,12},{12,0},{1,5},{5,9},{9,13},{13,1},{2,6},{6,10},{... | collective-permute-start | bytes 6152 | tf_op jit(solution)/shard_map/ppermute | solution.py:28
  70.1 65.6 %collective-permute-start.5 = (f32[1,4,128]{2,1,0:T(4,128)S(1)}, f32[1,4,128]{2,1,0:T(4,128)S(1)}, u32[]{:S(2)}, u32[]{:S(2)}) collective-permute-start(f32[1,4,128]{2,1,0:T(4,128)S(1)} %get-tuple-element.1814), channel_id=1, source_target_pairs={{4,0},{8,4},{12,8},{0,12},{5,1},{9,5},{13,9},{1,13},{6,2},{10,6},{... | collective-permute-start | bytes 6152 | tf_op jit(solution)/shard_map/ppermute | solution.py:30
  135.6 31.0 %copy-start.4 = (f32[1024]{0:T(1024)}, f32[1024]{0:T(1024)S(1)}, u32[]{:S(2)}) copy-start(f32[1024]{0:T(1024)S(1)} %get-tuple-element.2483) | copy-start | bytes 12292
  135.7 3.1 %collective-permute-start.7 = (f32[4,1,128]{2,1,0:T(1,128)S(1)}, f32[4,1,128]{2,1,0:T(1,128)S(1)}, u32[]{:S(2)}, u32[]{:S(2)}) collective-permute-start(f32[4,1,128]{2,1,0:T(1,128)S(1)} %get-tuple-element.1809), channel_id=1, source_target_pairs={{0,1},{1,2},{2,3},{3,0},{4,5},{5,6},{6,7},{7,4},{8,9},{9,10},{10,1... | collective-permute-start | bytes 6152 | tf_op jit(solution)/shard_map/ppermute | solution.py:28
  135.8 3.0 %collective-permute-start.6 = (f32[4,1,128]{2,1,0:T(1,128)S(1)}, f32[4,1,128]{2,1,0:T(1,128)S(1)}, u32[]{:S(2)}, u32[]{:S(2)}) collective-permute-start(f32[4,1,128]{2,1,0:T(1,128)S(1)} %get-tuple-element.1810), channel_id=1, source_target_pairs={{1,0},{2,1},{3,2},{0,3},{5,4},{6,5},{7,6},{4,7},{9,8},{10,9},{11,1... | collective-permute-start | bytes 6152 | tf_op jit(solution)/shard_map/ppermute | solution.py:30
  155.8 3.1 %collective-permute-start.8 = (f32[1,4,128]{2,1,0:T(4,128)S(1)}, f32[1,4,128]{2,1,0:T(4,128)S(1)}, u32[]{:S(2)}, u32[]{:S(2)}) collective-permute-start(f32[1,4,128]{2,1,0:T(4,128)S(1)} %get-tuple-element.1794), channel_id=1, source_target_pairs={{0,3},{1,0},{2,1},{3,2},{4,7},{5,4},{6,5},{7,6},{8,11},{9,8},{10,9... | collective-permute-start | bytes 6152 | tf_op jit(solution)/shard_map/ppermute | solution.py:18
  157.8 3.1 %collective-permute-start.9 = (f32[1,4,128]{2,1,0:T(4,128)S(1)}, f32[1,4,128]{2,1,0:T(4,128)S(1)}, u32[]{:S(2)}, u32[]{:S(2)}) collective-permute-start(f32[1,4,128]{2,1,0:T(4,128)S(1)} %get-tuple-element.1793), channel_id=1, source_target_pairs={{0,1},{1,2},{2,3},{3,0},{4,5},{5,6},{6,7},{7,4},{8,9},{9,10},{10,1... | collective-permute-start | bytes 6152 | tf_op jit(solution)/shard_map/ppermute | solution.py:18
  160.9 3.6 %collective-permute-start.10 = (f32[1,4,128]{2,1,0:T(4,128)S(1)}, f32[1,4,128]{2,1,0:T(4,128)S(1)}, u32[]{:S(2)}, u32[]{:S(2)}) collective-permute-start(f32[1,4,128]{2,1,0:T(4,128)S(1)} %get-tuple-element.1808), channel_id=1, source_target_pairs={{0,12},{4,0},{8,4},{12,8},{1,13},{5,1},{9,5},{13,9},{2,14},{6,2},{... | collective-permute-start | bytes 6152 | tf_op jit(solution)/shard_map/ppermute | solution.py:18
  161.2 5.4 %collective-permute-start.11 = (f32[1,4,128]{2,1,0:T(4,128)S(1)}, f32[1,4,128]{2,1,0:T(4,128)S(1)}, u32[]{:S(2)}, u32[]{:S(2)}) collective-permute-start(f32[1,4,128]{2,1,0:T(4,128)S(1)} %get-tuple-element.1807), channel_id=1, source_target_pairs={{0,4},{4,8},{8,12},{12,0},{1,5},{5,9},{9,13},{13,1},{2,6},{6,10},{... | collective-permute-start | bytes 6152 | tf_op jit(solution)/shard_map/ppermute | solution.py:18
  177.0 1.4 collective-permute-start.12
  177.1 3.2 %collective-permute-start.13 = (f32[3,4,128]{2,0,1:T(4,128)S(1)}, f32[3,4,128]{2,0,1:T(4,128)S(1)}, u32[]{:S(2)}, u32[]{:S(2)}) collective-permute-start(f32[3,4,128]{2,0,1:T(4,128)S(1)} %get-tuple-element.1744), channel_id=1, source_target_pairs={{0,1},{1,2},{2,3},{3,0},{4,5},{5,6},{6,7},{7,4},{8,9},{9,10},{10,1... | collective-permute-start | bytes 18440 | tf_op jit(solution)/shard_map/ppermute | solution.py:18
  180.2 32.2 %collective-permute-start.14 = (f32[3,4,128]{2,0,1:T(4,128)S(1)}, f32[3,4,128]{2,0,1:T(4,128)S(1)}, u32[]{:S(2)}, u32[]{:S(2)}) collective-permute-start(f32[3,4,128]{2,0,1:T(4,128)S(1)} %get-tuple-element.1749), channel_id=1, source_target_pairs={{0,12},{4,0},{8,4},{12,8},{1,13},{5,1},{9,5},{13,9},{2,14},{6,2},{... | collective-permute-start | bytes 18440 | tf_op jit(solution)/shard_map/ppermute | solution.py:18
  210.3 49.2 %copy-start.5 = (s32[2,4,128]{2,1,0:T(4,128)S(1)}, s32[2,4,128]{2,1,0:T(4,128)}, u32[]{:S(2)}) copy-start(s32[2,4,128]{2,1,0:T(4,128)} %param.30) | copy-start | bytes 12292
  210.3 48.2 %reduce-scatter.9.cloned.1.call-start = ((), (), s32[]{:S(2)}) async-start(), calls=%async_computation.3 | async-start | bytes 327680
  210.4 26.8 %collective-permute-start.15 = (f32[3,4,128]{2,0,1:T(4,128)S(1)}, f32[3,4,128]{2,0,1:T(4,128)S(1)}, u32[]{:S(2)}, u32[]{:S(2)}) collective-permute-start(f32[3,4,128]{2,0,1:T(4,128)S(1)} %get-tuple-element.1748), channel_id=1, source_target_pairs={{0,4},{4,8},{8,12},{12,0},{1,5},{5,9},{9,13},{13,1},{2,6},{6,10},{... | collective-permute-start | bytes 18440 | tf_op jit(solution)/shard_map/ppermute | solution.py:18
Sparse Core Ops, SparseCore 0:
  210.4 26.7 reduce-scatter.6
  239.8 18.7 reduce-scatter.8
where the time goes:
time: 268 us; the launch traced here: 267 us
  other arithmetic  146 us (54%)
  waiting for transfers between devices  57.1 us (21%)
  starting transfers between devices  19.6 us (7%)
  blocking collectives  18.3 us (7%)
  between operations  15.6 us (6%)
  local copies, waits for them, and re-layouts  6.67 us (2%)
  matrix products  3.78 us (1%)
    reduce_sum x4, other arithmetic, centre_distance(): apart_axis = flat_pos[axis_slot][:, None] - centre[axis_slot][None, :]  59 us
    unnamed x4, waiting for transfers between devices  46.1 us
    reduce_sum x2, other arithmetic, potential_block(): product = flat_born[:, None] * comp_radius[None, :]  28.8 us
    reduce_sum x8, other arithmetic, pair_distance(): own_pos[axis_slot][..., :, None] - part_pos[axis_slot][..., None, :]  25.1 us
    reduce_sum x2, other arithmetic, screen_block(): jnp.sum(jnp.where(keep, volume * weight / (denom_sq * denom_sq), 0.0), ax...  19.9 us
    all_gather x1, blocking collectives, local(): all_table = lax.all_gather(sub_table, 'dom', axis=1, tiled=True)  13.1 us
    ppermute x4, starting transfers between devices, extended(): lax.ppermute(head, axis, [((i + 1) % count, i) for i in range(count)])  9.21 us
    ppermute x8, waiting for transfers between devices, passed_along(): lax.ppermute(shard, axis, [(i, (i + by) % size) for i in range(size)])  9.12 us
  transfers between devices with their start and end apart: 18, of which 10 were waited for; matrix products, arithmetic and copies ran while one was open for 46% of the time, Pallas kernels for 0%

commit v1 on v0

v1 whole, which is shorter than its diff:
```python
import jax
import jax.numpy as jnp
from jax import lax
from jax.experimental import pallas as pl
from jax.experimental.pallas import tpu as pltpu
from jax.sharding import PartitionSpec as P

CT = 16
LANES = 128
SUBLANES = 8
WIDE = 2
SPAN = 64.0
RADIUS_FACTOR = 1.5
LOG2E = 1.4426950408889634
LN2 = 0.6931471805599453
HIGHEST = lax.Precision.HIGHEST
AXES = ("dom", "sub")
STEPS = ((-1, -1), (-1, 0), (-1, 1), (0, -1), (0, 1), (1, -1), (1, 0), (1, 1))
SELF = len(STEPS)
NEAR = len(STEPS) + 1


def side_tiles(rz, rs, rows, cols):
    along = {0: range(rows), 1: [rows - 1], -1: [0]}[rz]
    around = {0: range(cols), 1: [cols - 1], -1: [0]}[rs]
    return [(a, b) for a in along for b in around]


def partner(a, b, k, rows, cols):
    dz, ds = STEPS[k] if k < SELF else (0, 0)
    az, bs = a + dz, b + ds
    rz = -1 if az < 0 else 1 if az >= rows else 0
    rs = -1 if bs < 0 else 1 if bs >= cols else 0
    tile = (az % rows, bs % cols)
    if rz == 0 and rs == 0:
        return (0, 0), None, tile
    return (rz, rs), side_tiles(-rz, -rs, rows, cols).index(tile), tile


def device_at(rz, rs, dom_count, sub_count):
    along = jnp.clip(lax.axis_index("dom") + rz, 0, dom_count - 1)
    around = lax.rem(lax.axis_index("sub") + rs + sub_count, sub_count)
    return along * sub_count + around


def in_range(rz, dom_count):
    at = lax.axis_index("dom") + rz
    return (at >= 0) & (at < dom_count)


def far_unroll(devices):
    return 16 if devices % 16 == 0 else 1


def member_table(seg_ref, a, b, cols):
    comp = lax.broadcasted_iota(jnp.int32, (LANES, LANES), 0)
    owner = seg_ref[a, b : b + 1, :] + (a * cols + b) * CT
    return (comp == owner).astype(jnp.float32)


def turned(row):
    block = jnp.broadcast_to(row, (LANES, LANES)).T
    return block.reshape(LANES // SUBLANES, SUBLANES, LANES)


def lane_sums(block):
    return jnp.sum(block.reshape(LANES, LANES).T, axis=0, keepdims=True)


def pack_body(dims, pos_ref, q_ref, r_ref, seg_ref, send_ref, members_ref):
    rows, cols, dom_count, sub_count = dims
    slots = max(rows, cols)
    total = jnp.zeros((SUBLANES, LANES), jnp.float32)
    one = jnp.ones((1, LANES), jnp.float32)
    for a in range(rows):
        for b in range(cols):
            at = slice(b, b + 1)
            rho = r_ref[a, at, :]
            values = jnp.concatenate(
                [pos_ref[0, a, at, :], pos_ref[1, a, at, :], pos_ref[2, a, at, :],
                 q_ref[a, at, :], rho * rho * rho, rho, one, one], axis=0)
            total = total + lax.dot_general(
                values, member_table(seg_ref, a, b, cols), (((1,), (1,)), ((), ())),
                precision=HIGHEST, preferred_element_type=jnp.float32)
    members = total[6:7]
    comp_radius = RADIUS_FACTOR * total[5:6] / members
    table = jnp.concatenate(
        [total[0:3] / members, total[3:5], comp_radius, (-0.25 * LOG2E) / comp_radius,
         comp_radius * comp_radius], axis=0)
    members_ref[...] = jnp.broadcast_to(members, (SUBLANES, LANES))

    def put(d, carry):
        send_ref[d, 0:8, :] = table
        return carry

    lax.fori_loop(0, dom_count * sub_count, put, 0)
    for rz in (-1, 0, 1):
        for rs in (-1, 0, 1):
            where = device_at(rz, rs, dom_count, sub_count)

            @pl.when(in_range(rz, dom_count))
            def _(rz=rz, rs=rs, where=where):
                for slot, (a, b) in enumerate(side_tiles(rz, rs, rows, cols)[:slots]):
                    at = slice(b, b + 1)
                    for c in range(3):
                        line = 8 + c * slots + slot
                        send_ref[where, line : line + 1, :] = pos_ref[c, a, at, :]
                    line = 8 + 3 * slots + slot
                    send_ref[where, line : line + 1, :] = r_ref[a, at, :]


def near_row(dims, k, a, b, recv_ref, own, base, c):
    rows, cols, dom_count, sub_count = dims
    slots = max(rows, cols)
    (rz, rs), slot, (pa, pb) = partner(a, b, k, rows, cols)
    if slot is None:
        return own(c, pa, pb)
    line = base + c * slots + slot
    return recv_ref[device_at(rz, rs, dom_count, sub_count), line : line + 1, :]


def mask_rows(dims, near_ref, table_ref):
    rows, cols, dom_count, sub_count = dims
    tile_of = lax.broadcasted_iota(jnp.int32, (1, LANES), 1) // CT
    for a in range(rows):
        for b in range(cols):
            t = a * cols + b
            for k in range(NEAR):
                (rz, rs), _, (pa, pb) = partner(a, b, k, rows, cols)
                where = device_at(rz, rs, dom_count, sub_count)
                struck = tile_of == pa * cols + pb
                if k < SELF:
                    struck = struck & (near_ref[a, b, k] == 1)
                kept = table_ref[where, t : t + 1, :]
                table_ref[where, t : t + 1, :] = jnp.where(struck, 0.0, kept)


def spread(ref, lead, line):
    return ref[lead, pl.ds(line, SUBLANES, stride=0), :]


def own_pair_mask(g, t, v):
    atom = (g * WIDE + v - t * (LANES // SUBLANES)) * SUBLANES
    atom = atom + lax.broadcasted_iota(jnp.int32, (SUBLANES, LANES), 0)
    return atom == lax.broadcasted_iota(jnp.int32, (SUBLANES, LANES), 1)


def screen_body(dims, near_ref, recv_ref, pos_ref, q_ref, r_ref, born_ref, send_ref,
                turned_ref, near_tab, far_vol, sums_ref):
    rows, cols, dom_count, sub_count = dims
    devices = dom_count * sub_count
    slots = max(rows, cols)
    per_tile = LANES // SUBLANES

    def own(c, a, b):
        if c < 3:
            return pos_ref[c, a, b : b + 1, :]
        return r_ref[a, b : b + 1, :]

    def put(d, carry):
        far_vol[d] = jnp.broadcast_to(recv_ref[d, 4:5, :], (rows * cols, LANES))
        return carry

    lax.fori_loop(0, devices, put, 0)
    mask_rows(dims, near_ref, far_vol)
    for a in range(rows):
        for b in range(cols):
            t = a * cols + b
            for c in range(3):
                turned_ref[c, t * per_tile : (t + 1) * per_tile] = turned(own(c, a, b))
            for k in range(NEAR):
                x, y, z, rho = [near_row(dims, k, a, b, recv_ref, own, 8, c) for c in range(4)]
                volume = rho * rho * rho
                if k < SELF:
                    volume = jnp.where(near_ref[a, b, k] == 1, volume, 0.0)
                near_tab[t * NEAR + k, 0:1, :] = x
                near_tab[t * NEAR + k, 1:2, :] = y
                near_tab[t * NEAR + k, 2:3, :] = z
                near_tab[t * NEAR + k, 3:4, :] = rho * rho
                near_tab[t * NEAR + k, 4:5, :] = volume

    unroll = far_unroll(devices)

    def group(g, carry):
        t = g // (per_tile // WIDE)
        own_at = [[turned_ref[c, g * WIDE + v] for c in range(3)] for v in range(WIDE)]

        def dist(v, x, y, z):
            dx, dy, dz = own_at[v][0] - x, own_at[v][1] - y, own_at[v][2] - z
            return dx * dx + dy * dy + dz * dz

        sums = [jnp.zeros((SUBLANES, LANES), jnp.float32) for _ in range(WIDE)]
        for k in range(NEAR):
            x, y, z, rho_sq, volume = [spread(near_tab, t * NEAR + k, c) for c in range(5)]
            for v in range(WIDE):
                vol = jnp.where(own_pair_mask(g, t, v), 0.0, volume) if k == SELF else volume
                d = dist(v, x, y, z) + rho_sq
                sums[v] = sums[v] + vol / (d * d)

        def chunk(n, sums):
            sums = list(sums)
            for j in range(unroll):
                d = n * unroll + j
                x, y, z = [spread(recv_ref, d, c) for c in range(3)]
                rho_sq = spread(recv_ref, d, 7)
                volume = spread(far_vol, d, t)
                for v in range(WIDE):
                    s = dist(v, x, y, z)
                    near = s + rho_sq
                    sums[v] = sums[v] + volume * s / ((s + SPAN) * (near * near))
            return tuple(sums)

        sums = lax.fori_loop(0, devices // unroll, chunk, tuple(sums))
        for v in range(WIDE):
            sums_ref[g * WIDE + v] = sums[v]
        return carry

    lax.fori_loop(0, rows * cols * per_tile // WIDE, group, 0)
    for a in range(rows):
        for b in range(cols):
            t = a * cols + b
            screening = lane_sums(sums_ref[t * per_tile : (t + 1) * per_tile])
            rho = r_ref[a, b : b + 1, :]
            born_ref[a, b : b + 1, :] = rho * (1.0 + rho * screening)
    for rz in (-1, 0, 1):
        for rs in (-1, 0, 1):
            where = device_at(rz, rs, dom_count, sub_count)

            @pl.when(in_range(rz, dom_count))
            def _(rz=rz, rs=rs, where=where):
                for slot, (a, b) in enumerate(side_tiles(rz, rs, rows, cols)[:slots]):
                    send_ref[where, slot : slot + 1, :] = born_ref[a, b : b + 1, :]
                    line = slots + slot
                    send_ref[where, line : line + 1, :] = q_ref[a, b : b + 1, :]


def energy_body(dims, near_ref, recv_ref, halo_ref, pos_ref, q_ref, r_ref, born_ref,
                rgrad_ref, grad_ref, send_ref,
                turned_ref, near_tab, far_vol, far_q, pair_f, pair_s, far_acc, near_acc,
                sums_ref, rg_turned):
    rows, cols, dom_count, sub_count = dims
    devices = dom_count * sub_count
    slots = max(rows, cols)
    tiles = rows * cols
    per_tile = LANES // SUBLANES

    def own(c, a, b):
        at = slice(b, b + 1)
        if c < 3:
            return pos_ref[c, a, at, :]
        return r_ref[a, at, :]

    def own_late(c, a, b):
        at = slice(b, b + 1)
        return born_ref[a, at, :] if c == 0 else q_ref[a, at, :]

    zero = jnp.zeros((SUBLANES, LANES), jnp.float32)

    def put(d, carry):
        far_vol[d] = jnp.broadcast_to(recv_ref[d, 4:5, :], (tiles, LANES))
        far_q[d] = jnp.broadcast_to(0.5 * recv_ref[d, 3:4, :], (tiles, LANES))
        for c in range(3):
            far_acc[d, c] = zero
        return carry

    lax.fori_loop(0, devices, put, 0)
    mask_rows(dims, near_ref, far_vol)
    mask_rows(dims, near_ref, far_q)
    for a in range(rows):
        for b in range(cols):
            t = a * cols + b
            at = slice(b, b + 1)
            own_rows = [own(0, a, b), own(1, a, b), own(2, a, b), born_ref[a, at, :],
                        q_ref[a, at, :], r_ref[a, at, :]]
            for c, row in enumerate(own_rows):
                turned_ref[c, t * per_tile : (t + 1) * per_tile] = turned(row)
            for k in range(NEAR):
                x, y, z, rho = [near_row(dims, k, a, b, recv_ref, own, 8, c) for c in range(4)]
                born, charge = [near_row(dims, k, a, b, halo_ref, own_late, 0, c) for c in range(2)]
                volume = rho * rho * rho
                charge = 0.5 * charge
                if k < SELF:
                    flagged = near_ref[a, b, k] == 1
                    volume = jnp.where(flagged, volume, 0.0)
                    charge = jnp.where(flagged, charge, 0.0)
                lines = [x, y, z, born, (-0.25 * LOG2E) / born, charge, rho * rho, volume]
                for c, row in enumerate(lines):
                    near_tab[t * NEAR + k, c : c + 1, :] = row
                for c in range(3):
                    near_acc[t * NEAR + k, c] = zero

    unroll = far_unroll(devices)
    trips = devices // unroll

    def group(g, carry):
        t = g // (per_tile // WIDE)
        mine = [[turned_ref[c, g * WIDE + v] for c in range(6)] for v in range(WIDE)]
        inverse = [1.0 / mine[v][3] for v in range(WIDE)]

        def apart(v, x, y, z):
            return mine[v][0] - x, mine[v][1] - y, mine[v][2] - z

        def pair(v, x, y, z, other_born, other_inv):
            dx, dy, dz = apart(v, x, y, z)
            s = dx * dx + dy * dy + dz * dz
            power = s * (inverse[v] * other_inv)
            e = jnp.exp2(power)
            pe = (mine[v][3] * other_born) * e
            r = lax.rsqrt(s + pe)
            return s, 1.0 - LN2 * power, 1.0 - 0.25 * e, pe, r, r * r

        born_near = [zero] * WIDE
        for k in range(NEAR):
            x, y, z, other, other_inv, charge = [
                spread(near_tab, t * NEAR + k, c) for c in range(6)]
            for v in range(WIDE):
                s, grow, fade, pe, r, rr = pair(v, x, y, z, other, other_inv)
                q = jnp.where(own_pair_mask(g, t, v), 0.0, charge) if k == SELF else charge
                h = (q * (mine[v][4] * r)) * rr
                pair_f[devices + k, v] = h * fade
                pair_s[devices + k, v] = s
                born_near[v] = born_near[v] + (h * pe) * grow

        def far_energy(n, born_far):
            born_far = list(born_far)
            for j in range(unroll):
                d = n * unroll + j
                x, y, z = [spread(recv_ref, d, c) for c in range(3)]
                other, other_inv = spread(recv_ref, d, 5), spread(recv_ref, d, 6)
                charge = spread(far_q, d, t)
                for v in range(WIDE):
                    s, grow, fade, pe, r, rr = pair(v, x, y, z, other, other_inv)
                    inv = 1.0 / (s + SPAN)
                    qr = charge * (mine[v][4] * r)
                    wr = (s * inv) * rr
                    pair_f[d, v] = qr * (wr * fade - (2.0 * SPAN) * (inv * inv))
                    pair_s[d, v] = s
                    born_far[v] = born_far[v] + qr * ((wr * pe) * grow)
            return tuple(born_far)

        born_far = lax.fori_loop(0, trips, far_energy, tuple([zero] * WIDE))

        scale = []
        for v in range(WIDE):
            part = inverse[v] * (0.5 * born_far[v] + born_near[v])
            own_part = mine[v][4] * inverse[v]
            rg = jnp.sum(part, axis=1, keepdims=True) + 0.5 * (own_part * own_part)
            rg_turned[g * WIDE + v] = rg
            scale.append(4.0 * rg * (mine[v][5] * mine[v][5]))

        own_grad = [[zero] * 3 for _ in range(WIDE)]
        for k in range(NEAR):
            j = t * NEAR + k
            x, y, z = [spread(near_tab, j, c) for c in range(3)]
            rho_sq, volume = spread(near_tab, j, 6), spread(near_tab, j, 7)
            other_grad = [zero] * 3
            for v in range(WIDE):
                inv = 1.0 / (pair_s[devices + k, v] + rho_sq)
                f = pair_f[devices + k, v] - (scale[v] * volume) * (inv * inv * inv)
                for c, delta in enumerate(apart(v, x, y, z)):
                    part = f * delta
                    own_grad[v][c] = own_grad[v][c] + part
                    other_grad[c] = other_grad[c] + part
            for c in range(3):
                near_acc[j, c] = near_acc[j, c] + other_grad[c]

        def far_chain(n, flat):
            own_grad = [list(flat[3 * v : 3 * v + 3]) for v in range(WIDE)]
            for j in range(unroll):
                d = n * unroll + j
                x, y, z = [spread(recv_ref, d, c) for c in range(3)]
                rho_sq = spread(recv_ref, d, 7)
                volume = spread(far_vol, d, t)
                other_grad = [zero] * 3
                for v in range(WIDE):
                    s = pair_s[d, v]
                    wide, near = s + SPAN, s + rho_sq
                    inv = 1.0 / (wide * near)
                    slope = (0.5 * SPAN * near - s * wide) * ((inv * inv) * (inv * wide))
                    f = pair_f[d, v] + (scale[v] * volume) * slope
                    for c, delta in enumerate(apart(v, x, y, z)):
                        part = f * delta
                        own_grad[v][c] = own_grad[v][c] + part
                        other_grad[c] = other_grad[c] + part
                for c in range(3):
                    far_acc[d, c] = far_acc[d, c] + other_grad[c]
            return tuple(own_grad[v][c] for v in range(WIDE) for c in range(3))

        flat = lax.fori_loop(
            0, trips, far_chain, tuple(own_grad[v][c] for v in range(WIDE) for c in range(3)))
        for v in range(WIDE):
            for c in range(3):
                sums_ref[c, g * WIDE + v] = flat[3 * v + c]
        return carry

    lax.fori_loop(0, tiles * per_tile // WIDE, group, 0)

    def send_far(d, carry):
        for c in range(3):
            send_ref[d, c : c + 1, :] = -jnp.sum(far_acc[d, c], axis=0, keepdims=True)
        return carry

    lax.fori_loop(0, devices, send_far, 0)
    owed = {}
    for a in range(rows):
        for b in range(cols):
            for k in range(NEAR):
                rel, slot, tile = partner(a, b, k, rows, cols)
                key = (rel, slot) if slot is not None else tile
                owed.setdefault(key, []).append((a * cols + b) * NEAR + k)

    def partner_sum(places, c):
        total = near_acc[places[0], c]
        for place in places[1:]:
            total = total + near_acc[place, c]
        return jnp.sum(total, axis=0, keepdims=True)

    for a in range(rows):
        for b in range(cols):
            t = a * cols + b
            at = slice(t * per_tile, (t + 1) * per_tile)
            rgrad_ref[a, b : b + 1, :] = rg_turned[at].reshape(LANES, LANES).T[0:1]
            for c in range(3):
                grad_ref[c, a, b : b + 1, :] = (
                    lane_sums(sums_ref[c, at]) - partner_sum(owed[(a, b)], c))
    for rz in (-1, 0, 1):
        for rs in (-1, 0, 1):
            if rz == 0 and rs == 0:
                continue
            where = device_at(rz, rs, dom_count, sub_count)

            @pl.when(in_range(rz, dom_count))
            def _(rz=rz, rs=rs, where=where):
                for slot in range(len(side_tiles(rz, rs, rows, cols))):
                    for c in range(3):
                        line = 3 + c * slots + slot
                        send_ref[where, line : line + 1, :] = -partner_sum(
                            owed[((rz, rs), slot)], c)


def finish_body(dims, recv_ref, grad_ref, members_ref, seg_ref, force_ref):
    rows, cols, dom_count, sub_count = dims
    slots = max(rows, cols)

    def add(d, total):
        return total + recv_ref[d, 0:3, :]

    centre_grad = lax.fori_loop(
        0, dom_count * sub_count, add, jnp.zeros((3, LANES), jnp.float32))
    per_member = centre_grad / members_ref[0:3, :]
    per_member = jnp.concatenate([per_member, jnp.zeros((5, LANES), jnp.float32)], axis=0)
    for a in range(rows):
        for b in range(cols):
            spread_out = lax.dot_general(
                per_member, member_table(seg_ref, a, b, cols), (((1,), (0,)), ((), ())),
                precision=HIGHEST, preferred_element_type=jnp.float32)
            for c in range(3):
                force_ref[c, a, b : b + 1, :] = -(
                    grad_ref[c, a, b : b + 1, :] + spread_out[c : c + 1])
    for rz in (-1, 0, 1):
        for rs in (-1, 0, 1):
            if rz == 0 and rs == 0:
                continue
            where = device_at(rz, rs, dom_count, sub_count)

            @pl.when(in_range(rz, dom_count))
            def _(rz=rz, rs=rs, where=where):
                for slot, (a, b) in enumerate(side_tiles(rz, rs, rows, cols)):
                    for c in range(3):
                        line = 3 + c * slots + slot
                        force_ref[c, a, b : b + 1, :] = (
                            force_ref[c, a, b : b + 1, :] - recv_ref[where, line : line + 1, :])


def f32(*shape):
    return jax.ShapeDtypeStruct(shape, jnp.float32)


def local(positions, charge, radius, segment, near_tiles):
    rows, cols, width = charge.shape
    dom_count, sub_count = lax.axis_size("dom"), lax.axis_size("sub")
    dims = (rows, cols, dom_count, sub_count)
    devices = dom_count * sub_count
    tiles = rows * cols
    assert width == LANES and tiles * CT == LANES and sub_count > 2
    slots = max(rows, cols)
    vectors = tiles * LANES // SUBLANES
    vmem = pltpu.MemorySpace.VMEM
    vec = (SUBLANES, LANES)

    def call(body, ins, outs, scratch=()):
        return pl.pallas_call(
            lambda *refs: body(dims, *refs),
            out_shape=outs,
            in_specs=[pl.BlockSpec(memory_space=pltpu.MemorySpace.SMEM if x is near_tiles else vmem)
                      for x in ins],
            out_specs=[pl.BlockSpec(memory_space=vmem) for _ in outs],
            scratch_shapes=list(scratch),
            compiler_params=pltpu.CompilerParams(vmem_limit_bytes=48 << 20),
            name=body.__name__,
        )(*ins)

    def exchanged(blocks):
        return lax.all_to_all(blocks, AXES, 0, 0, tiled=True)

    send, members = call(
        pack_body, (positions, charge, radius, segment),
        [f32(devices, 8 + 4 * slots, LANES), f32(*vec)])
    table = exchanged(send)
    born_radii, send = call(
        screen_body, (near_tiles, table, positions, charge, radius),
        [f32(rows, cols, LANES), f32(devices, 2 * slots, LANES)],
        [pltpu.VMEM((3, vectors) + vec, jnp.float32),
         pltpu.VMEM((tiles * NEAR,) + vec, jnp.float32),
         pltpu.VMEM((devices, tiles, LANES), jnp.float32),
         pltpu.VMEM((vectors,) + vec, jnp.float32)])
    halo = exchanged(send)
    radius_grad, grad, send = call(
        energy_body, (near_tiles, table, halo, positions, charge, radius, born_radii),
        [f32(rows, cols, LANES), f32(3, rows, cols, LANES), f32(devices, 4 + 3 * slots, LANES)],
        [pltpu.VMEM((6, vectors) + vec, jnp.float32),
         pltpu.VMEM((tiles * NEAR,) + vec, jnp.float32),
         pltpu.VMEM((devices, tiles, LANES), jnp.float32),
         pltpu.VMEM((devices, tiles, LANES), jnp.float32),
         pltpu.VMEM((devices + NEAR, WIDE) + vec, jnp.float32),
         pltpu.VMEM((devices + NEAR, WIDE) + vec, jnp.float32),
         pltpu.VMEM((devices, 3) + vec, jnp.float32),
         pltpu.VMEM((tiles * NEAR, 3) + vec, jnp.float32),
         pltpu.VMEM((3, vectors) + vec, jnp.float32),
         pltpu.VMEM((vectors,) + vec, jnp.float32)])
    back = exchanged(send)
    forces = call(
        finish_body, (back, grad, members, segment), [f32(3, rows, cols, LANES)])[0]
    return born_radii, radius_grad, forces


def solution(mesh):
    flat = P(("groups", "dom"), "sub", None)
    stacked = P(None, ("groups", "dom"), "sub", None)
    return jax.shard_map(
        local,
        mesh=mesh,
        in_specs=(stacked, flat, flat, flat, flat),
        out_specs=(flat, flat, stacked),
        check_vma=False,
    )
```

time: 268 us -> 81.6 us (0.30)
  other arithmetic: 146 us -> 0 us
  waiting for transfers between devices: 57.1 us -> 0 us
  Pallas kernels: 0 us -> 41.3 us
  starting transfers between devices: 19.6 us -> 0 us
  blocking collectives: 18.3 us -> 36.4 us
  between operations: 15.6 us -> 0.66 us
  local copies, waits for them, and re-layouts: 6.67 us -> 2.77 us
  matrix products: 3.78 us -> 0 us
    reduce_sum x21 -> x0, other arithmetic: 137 us -> none  [the longest x4 59 us: centre_distance(): apart_axis = flat_pos[axis_slot][:, None] - centre[axis_slot][None, :]]
    unnamed x4 -> x0, waiting for transfers between devices: 46.1 us -> none
    pallas_call x0 -> x4, Pallas kernels: none -> 41.3 us  [call(): pl.pallas_call(lambda *refs: body(dims, *refs), out_shape=outs, in_specs=...]
    all_to_all x0 -> x3, blocking collectives: none -> 36.4 us  [exchanged(): return lax.all_to_all(blocks, AXES, 0, 0, tiled=True)]
    ppermute x16 -> x0, starting transfers between devices: 19.5 us -> none  [the longest x4 9.21 us: extended(): lax.ppermute(head, axis, [((i + 1) % count, i) for i in range(count)])]
    all_gather x2 -> x0, blocking collectives: 18.3 us -> none  [the longest x1 13.1 us: local(): all_table = lax.all_gather(sub_table, 'dom', axis=1, tiled=True)]
    ppermute x16 -> x0, waiting for transfers between devices: 11 us -> none  [the longest x8 9.12 us: passed_along(): lax.ppermute(shard, axis, [(i, (i + by) % size) for i in range(size)])]
    dot_general x5 -> x0, matrix products: 3.78 us -> none  [the longest x1 0.9 us: components(): jnp.einsum('kabl,ablc->kabc', positions, onehot, precision=highest)]
  transfers between devices with their start and end apart: 18 -> 0, of which waited for: 10 -> 0; matrix products, arithmetic and copies ran while one was open for 46% -> 0% of each run, Pallas kernels for 0% -> 0%
where the time goes in v1:
time: 81.6 us; the launch traced here: 81.2 us
  Pallas kernels  41.3 us (51%)
  blocking collectives  36.4 us (45%)
  local copies, waits for them, and re-layouts  2.77 us (3%)
    pallas_call x4, Pallas kernels, call(): pl.pallas_call(lambda *refs: body(dims, *refs), out_shape=outs, in_specs=...  41.3 us
    all_to_all x3, blocking collectives, exchanged(): return lax.all_to_all(blocks, AXES, 0, 0, tiled=True)  36.4 us
    unnamed x14, local copies, waits for them, and re-layouts  2.77 us

profile of v1, /device:TPU:0, one launch (start us, length us, event | category | flops | bytes accessed | tf_op | source)
XLA Modules:
  0.0 81.2 jit_solution(8294117296234018312)
XLA Ops:
  0.6 0.0 copy-start
  0.6 0.7 copy-done
  1.3 0.0 copy-start.1
  1.3 0.7 copy-done.1
  2.0 0.0 copy-start.2
  2.0 0.7 copy-done.2
  2.7 0.0 copy-start.4
  2.7 0.7 copy-done.4
  3.4 1.1 %pack_body.1 = (f32[16,24,128]{2,1,0:T(8,128)S(1)}, f32[8,128]{1,0:T(8,128)S(1)}) custom-call(f32[3,2,4,128]{3,2,1,0:T(4,128)S(1)} %copy-done, f32[2,4,128]{2,1,0:T(4,128)S(1)} %copy-done.1, f32[2,4,128]{2,1,0:T(4,128)S(1)} %copy-done.2, s32[2,4,128]{2,1,0:T(4,128)S(1)} %copy-done.4), custom_call_target="tpu_custom_call" | custom-call | tf_op jit(solution)/shard_map/pack_body/pallas_call | solution.py:492
  4.5 0.0 copy-start.3
  4.5 16.2 %all_to_all.15.refs_1_ = f32[16,24,128]{2,1,0:T(8,128)S(1)} all-to-all(f32[16,24,128]{2,1,0:T(8,128)S(1)} %get-tuple-element.10), channel_id=1, replica_groups=mesh['groups'=2,'dom'=4,'sub'=4] {'dom','sub'}, dimensions={0} | all-to-all | bytes 393216 | tf_op jit(solution)/shard_map/all_to_all | solution.py:504
  20.6 0.0 copy-done.3
  20.6 9.3 %screen_body.1 = (f32[2,4,128]{2,1,0:T(4,128)}, f32[16,8,128]{2,1,0:T(8,128)S(1)}) custom-call(s32[2,4,8]{2,1,0:T(4,128)S(1)} %copy-done.3, f32[16,24,128]{2,1,0:T(8,128)S(1)} %all_to_all.15.refs_1_, f32[3,2,4,128]{3,2,1,0:T(4,128)S(1)} %copy-done, f32[2,4,128]{2,1,0:T(4,128)S(1)} %copy-done.1, f32[2,4,128]{2,1,0:T(4,128)S(1)} %copy-done.2), custom_call_target="tpu_custom_call" | custom-call | tf_op jit(solution)/shard_map/screen_body/pallas_call | solution.py:492
  30.0 0.0 copy-start.6
  30.0 9.6 %all_to_all.16.refs_2_ = f32[16,8,128]{2,1,0:T(8,128)S(1)} all-to-all(f32[16,8,128]{2,1,0:T(8,128)S(1)} %get-tuple-element.12), channel_id=1, replica_groups=mesh['groups'=2,'dom'=4,'sub'=4] {'dom','sub'}, dimensions={0} | all-to-all | bytes 131072 | tf_op jit(solution)/shard_map/all_to_all | solution.py:504
  39.6 0.0 copy-done.6
  39.6 29.7 %energy_body.1 = (f32[2,4,128]{2,1,0:T(4,128)}, f32[3,2,4,128]{3,2,1,0:T(4,128)S(1)}, f32[16,16,128]{2,1,0:T(8,128)S(1)}) custom-call(s32[2,4,8]{2,1,0:T(4,128)S(1)} %copy-done.3, f32[16,24,128]{2,1,0:T(8,128)S(1)} %all_to_all.15.refs_1_, f32[16,8,128]{2,1,0:T(8,128)S(1)} %all_to_all.16.refs_2_, f32[3,2,4,128]{3,2,1,0:T(4,128)S(1)} %copy-done, ...), custom_call_target="tpu_custom_call" | custom-call | tf_op jit(solution)/shard_map/energy_body/pallas_call | solution.py:492
  69.3 0.0 copy-start.5
  69.3 10.6 %all_to_all.17.refs_0_ = f32[16,16,128]{2,1,0:T(8,128)S(1)} all-to-all(f32[16,16,128]{2,1,0:T(8,128)S(1)} %get-tuple-element.14), channel_id=1, replica_groups=mesh['groups'=2,'dom'=4,'sub'=4] {'dom','sub'}, dimensions={0} | all-to-all | bytes 262144 | tf_op jit(solution)/shard_map/all_to_all | solution.py:504
  79.9 0.0 copy-done.5
  79.9 1.2 %finish_body.1 = f32[3,2,4,128]{3,2,1,0:T(4,128)} custom-call(f32[16,16,128]{2,1,0:T(8,128)S(1)} %all_to_all.17.refs_0_, f32[3,2,4,128]{3,2,1,0:T(4,128)S(1)} %get-tuple-element.15.refs_1_, f32[8,128]{1,0:T(8,128)S(1)} %get-tuple-element.16.refs_2_, s32[2,4,128]{2,1,0:T(4,128)S(1)} %copy-done.5), custom_call_target="tpu_custom_call" | custom-call | tf_op jit(solution)/shard_map/finish_body/pallas_call | solution.py:492
Async XLA Ops:
  0.6 0.7 copy-start
  1.3 0.7 copy-start.1
  2.0 0.7 copy-start.2
  2.7 0.7 copy-start.4
  4.5 16.2 %copy-start.3 = (s32[2,4,8]{2,1,0:T(4,128)S(1)}, s32[2,4,8]{2,1,0:T(4,128)}, u32[]{:S(2)}) copy-start(s32[2,4,8]{2,1,0:T(4,128)} %refs_0_.5) | copy-start | bytes 772
  30.0 9.6 %copy-start.6 = (f32[2,4,128]{2,1,0:T(4,128)S(1)}, f32[2,4,128]{2,1,0:T(4,128)}, u32[]{:S(2)}) copy-start(f32[2,4,128]{2,1,0:T(4,128)} %get-tuple-element.7.refs_6_) | copy-start | bytes 12292
  69.3 10.6 %copy-start.5 = (s32[2,4,128]{2,1,0:T(4,128)S(1)}, s32[2,4,128]{2,1,0:T(4,128)}, u32[]{:S(2)}) copy-start(s32[2,4,128]{2,1,0:T(4,128)} %refs_3_.7) | copy-start | bytes 12292

commit v2 on v1

v2 whole, which is shorter than its diff:
```python
import jax
import jax.numpy as jnp
from jax import lax
from jax.experimental import pallas as pl
from jax.experimental.pallas import tpu as pltpu
from jax.sharding import PartitionSpec as P

CT = 16
LANES = 128
SUBLANES = 8
UNIT = 128.0
KROWS = 48
WROWS = 16
SPAN = 64.0
CHARGE_UNIT = 0.5 * UNIT ** -1.5
RADIUS_FACTOR = 1.5
LOG2E = 1.4426950408889634
LN2 = 0.6931471805599453
HIGHEST = lax.Precision.HIGHEST
AXES = ("dom", "sub")
STEPS = ((-1, -1), (-1, 0), (-1, 1), (0, -1), (0, 1), (1, -1), (1, 0), (1, 1))
SELF = len(STEPS)
NEAR = len(STEPS) + 1


def side_tiles(rz, rs, rows, cols):
    along = {0: range(rows), 1: [rows - 1], -1: [0]}[rz]
    around = {0: range(cols), 1: [cols - 1], -1: [0]}[rs]
    return [(a, b) for a in along for b in around]


def partner(a, b, k, rows, cols):
    dz, ds = STEPS[k] if k < SELF else (0, 0)
    az, bs = a + dz, b + ds
    rz = -1 if az < 0 else 1 if az >= rows else 0
    rs = -1 if bs < 0 else 1 if bs >= cols else 0
    tile = (az % rows, bs % cols)
    if rz == 0 and rs == 0:
        return (0, 0), None, tile
    return (rz, rs), side_tiles(-rz, -rs, rows, cols).index(tile), tile


def device_at(rz, rs, dom_count, sub_count):
    along = jnp.clip(lax.axis_index("dom") + rz, 0, dom_count - 1)
    around = lax.rem(lax.axis_index("sub") + rs + sub_count, sub_count)
    return along * sub_count + around


def in_range(rz, dom_count):
    at = lax.axis_index("dom") + rz
    return (at >= 0) & (at < dom_count)


def far_unroll(devices):
    return 16 if devices % 16 == 0 else 1


def pieces(value):
    first = value.astype(jnp.bfloat16).astype(jnp.float32)
    left = value - first
    second = left.astype(jnp.bfloat16).astype(jnp.float32)
    return first, second, left - second


def line_of(shape=(SUBLANES, LANES)):
    return lax.broadcasted_iota(jnp.int32, shape, 0)


def side_block(points, ones_line, norm_line, factor):
    norm = jnp.sum(points * points, axis=0, keepdims=True) * (1.0 / UNIT)
    line = line_of()
    block = jnp.where(line == norm_line, norm, jnp.where(line == ones_line, 1.0, factor * points))
    return pieces(block)


def weight_rows(first, second, third):
    rows = jnp.concatenate(
        [first, second[0:3], third[0:3], jnp.zeros((2, LANES), jnp.float32)], axis=0)
    return jnp.concatenate([rows, rows], axis=1).astype(jnp.bfloat16)


def other_tables(points):
    c1, c2, c3 = side_block(points, 4, 3, 1.0)
    table = jnp.concatenate([c1, c2, c1, c2, c3, c1], axis=0).astype(jnp.bfloat16)
    return table, weight_rows(c1, c2, c3)


def own_tables(points):
    x1, x2, x3 = side_block(points, 3, 4, -2.0 / UNIT)
    stack = jnp.concatenate(
        [x1, x1, x2, x2, x1, x3, jnp.zeros((LANES - KROWS, LANES), jnp.float32)], axis=0)
    w1, w2, w3 = side_block(points, 4, 3, 1.0)
    return stack.T[:, 0:KROWS].astype(jnp.bfloat16), weight_rows(w1, w2, w3)


def product(a, b):
    return jnp.dot(a, b, preferred_element_type=jnp.float32)


def product_turned(a, b):
    return lax.dot_general(a, b, (((1,), (1,)), ((), ())), preferred_element_type=jnp.float32)


def weighted(block):
    return block[4:5], block[0:3] + block[8:11] + block[11:14]


def member_table(seg_ref, a, b, cols):
    comp = lax.broadcasted_iota(jnp.int32, (LANES, LANES), 0)
    owner = seg_ref[a, b : b + 1, :] + (a * cols + b) * CT
    return (comp == owner).astype(jnp.float32)


def turned(row):
    return jnp.broadcast_to(row, (LANES, LANES)).T


def lane_sums(block):
    return jnp.sum(block.T, axis=0, keepdims=True)


def pack_body(dims, pos_ref, q_ref, r_ref, seg_ref, send_ref, members_ref):
    rows, cols, dom_count, sub_count = dims
    slots = max(rows, cols)
    total = jnp.zeros((SUBLANES, LANES), jnp.float32)
    one = jnp.ones((1, LANES), jnp.float32)
    for a in range(rows):
        for b in range(cols):
            at = slice(b, b + 1)
            rho = r_ref[a, at, :]
            values = jnp.concatenate(
                [pos_ref[0, a, at, :], pos_ref[1, a, at, :], pos_ref[2, a, at, :],
                 q_ref[a, at, :], rho * rho * rho, rho, one, one], axis=0)
            total = total + lax.dot_general(
                values, member_table(seg_ref, a, b, cols), (((1,), (1,)), ((), ())),
                precision=HIGHEST, preferred_element_type=jnp.float32)
    members = total[6:7]
    comp_radius = RADIUS_FACTOR * total[5:6] / members
    table = jnp.concatenate(
        [total[0:3] / members, CHARGE_UNIT * total[3:4], total[4:5],
         comp_radius * (1.0 / UNIT), (-0.25 * LOG2E * UNIT) / comp_radius,
         comp_radius * comp_radius * (1.0 / UNIT)], axis=0)
    members_ref[...] = jnp.broadcast_to(members, (SUBLANES, LANES))

    def put(d, carry):
        send_ref[d, 0:8, :] = table
        return carry

    lax.fori_loop(0, dom_count * sub_count, put, 0)
    for rz in (-1, 0, 1):
        for rs in (-1, 0, 1):
            where = device_at(rz, rs, dom_count, sub_count)

            @pl.when(in_range(rz, dom_count))
            def _(rz=rz, rs=rs, where=where):
                for slot, (a, b) in enumerate(side_tiles(rz, rs, rows, cols)[:slots]):
                    at = slice(b, b + 1)
                    for c in range(3):
                        line = 8 + c * slots + slot
                        send_ref[where, line : line + 1, :] = pos_ref[c, a, at, :]
                    line = 8 + 3 * slots + slot
                    send_ref[where, line : line + 1, :] = r_ref[a, at, :]


def mask_rows(dims, near_ref, table_ref):
    rows, cols, dom_count, sub_count = dims
    tile_of = lax.broadcasted_iota(jnp.int32, (1, LANES), 1) // CT
    for a in range(rows):
        for b in range(cols):
            t = a * cols + b
            for k in range(NEAR):
                (rz, rs), _, (pa, pb) = partner(a, b, k, rows, cols)
                where = device_at(rz, rs, dom_count, sub_count)
                struck = tile_of == pa * cols + pb
                if k < SELF:
                    struck = struck & (near_ref[a, b, k] == 1)
                kept = table_ref[where, t : t + 1, :]
                table_ref[where, t : t + 1, :] = jnp.where(struck, 0.0, kept)


def near_source(dims, rz, rs):
    rows, cols, dom_count, sub_count = dims
    return device_at(rz, rs, dom_count, sub_count)


def window_source(dims, place, recv_ref, own, base, c):
    rows, cols, _, _ = dims
    az, bs = place // (cols + 2) - 1, place % (cols + 2) - 1
    rz = -1 if az < 0 else 1 if az >= rows else 0
    rs = -1 if bs < 0 else 1 if bs >= cols else 0
    tile = (az % rows, bs % cols)
    if rz == 0 and rs == 0:
        return own(c, *tile)
    line = base + c * max(rows, cols) + side_tiles(-rz, -rs, rows, cols).index(tile)
    return recv_ref[near_source(dims, rz, rs), line : line + 1, :]


def window_place(t, k, cols):
    dz, ds = STEPS[k] if k < SELF else (0, 0)
    return (t // cols + 1 + dz) * (cols + 2) + t % cols + 1 + ds


def flagged(near_ref, t, k, cols, row):
    if k == SELF:
        return row
    return jnp.where(near_ref[t // cols, t % cols, k] == 1, row, 0.0)


def own_pair():
    shape = (LANES, LANES)
    return lax.broadcasted_iota(jnp.int32, shape, 0) == lax.broadcasted_iota(jnp.int32, shape, 1)


def over_far(devices, step, carry):
    unroll = far_unroll(devices)

    def chunk(n, carry):
        for j in range(unroll):
            carry = step(n * unroll + j, carry)
        return carry

    if devices == unroll:
        return chunk(0, carry)
    return lax.fori_loop(0, devices // unroll, chunk, carry)


def screen_body(dims, near_ref, recv_ref, pos_ref, q_ref, r_ref, born_ref, send_ref,
                own_k, own_w, win_k, win_w, win_c, win_r, far_k, far_w, far_c, far_vol):
    rows, cols, dom_count, sub_count = dims
    devices = dom_count * sub_count
    slots = max(rows, cols)
    line = line_of()

    middle = jnp.zeros((SUBLANES, LANES), jnp.float32)
    for c in range(3):
        mean = jnp.sum(pos_ref[c]) * (1.0 / (rows * cols * LANES))
        middle = jnp.where(line == c, mean, middle)

    def own(c, a, b):
        if c < 3:
            return pos_ref[c, a, b : b + 1, :]
        return r_ref[a, b : b + 1, :]

    def put(d, carry):
        far_vol[d] = jnp.broadcast_to(recv_ref[d, 4:5, :], (rows * cols, LANES))
        points = jnp.where(line < 3, recv_ref[d, 0:8, :] - middle, 0.0)
        far_c[d] = points
        far_k[d], far_w[d] = other_tables(points)
        return carry

    lax.fori_loop(0, devices, put, 0)
    mask_rows(dims, near_ref, far_vol)
    none = jnp.zeros((SUBLANES - 3, LANES), jnp.float32)
    for place in range((rows + 2) * (cols + 2)):
        x, y, z, rho = [window_source(dims, place, recv_ref, own, 8, c) for c in range(4)]
        points = jnp.concatenate([x, y, z, none], axis=0) - middle
        win_c[place] = points
        win_k[place], win_w[place] = other_tables(points)
        win_r[place, 0:1, :] = rho * rho * (1.0 / UNIT)
        win_r[place, 1:2, :] = rho * rho * rho
        az, bs = place // (cols + 2) - 1, place % (cols + 2) - 1
        if 0 <= az < rows and 0 <= bs < cols:
            own_k[az * cols + bs], own_w[az * cols + bs] = own_tables(points)

    def tile(t, carry):
        x = own_k[t]
        sums = jnp.zeros((LANES, LANES), jnp.float32)
        for k in range(NEAR):
            place = window_place(t, k, cols)
            volume = flagged(near_ref, t, k, cols, win_r[place, 1:2, :])
            if k == SELF:
                volume = jnp.where(own_pair(), 0.0, volume)
            near = product(x, win_k[place]) + win_r[place, 0:1, :]
            sums = sums + volume / (near * near)

        def far(d, sums):
            s = product(x, far_k[d])
            near = s + recv_ref[d, 7:8, :]
            volume = far_vol[d, pl.ds(t, 1), :]
            return sums + (volume * s) / ((s + SPAN / UNIT) * (near * near))

        sums = over_far(devices, far, sums)
        screening = lane_sums(sums) * (1.0 / (UNIT * UNIT))
        a, b = t // cols, t % cols
        rho = r_ref[a, pl.ds(b, 1), :]
        born_ref[a, pl.ds(b, 1), :] = rho * (1.0 + rho * screening)
        return carry

    lax.fori_loop(0, rows * cols, tile, 0)
    for rz in (-1, 0, 1):
        for rs in (-1, 0, 1):
            where = device_at(rz, rs, dom_count, sub_count)

            @pl.when(in_range(rz, dom_count))
            def _(rz=rz, rs=rs, where=where):
                for slot, (a, b) in enumerate(side_tiles(rz, rs, rows, cols)[:slots]):
                    send_ref[where, slot : slot + 1, :] = born_ref[a, b : b + 1, :]
                    line = slots + slot
                    send_ref[where, line : line + 1, :] = q_ref[a, b : b + 1, :]


def energy_body(dims, near_ref, recv_ref, halo_ref, q_ref, r_ref, born_ref,
                own_k, own_w, win_k, win_w, win_c, win_r, far_k, far_w, far_c, far_vol,
                rgrad_ref, grad_ref, send_ref,
                turned_ref, win_e, far_q, pair_f, pair_s, far_acc, win_acc):
    rows, cols, dom_count, sub_count = dims
    devices = dom_count * sub_count
    slots = max(rows, cols)
    tiles = rows * cols
    places = (rows + 2) * (cols + 2)

    def own(c, a, b):
        at = slice(b, b + 1)
        return born_ref[a, at, :] if c == 0 else q_ref[a, at, :]

    zero = jnp.zeros((LANES, LANES), jnp.float32)
    no_force = jnp.zeros((WROWS, LANES), jnp.float32)

    def put(d, carry):
        far_q[d] = jnp.broadcast_to(recv_ref[d, 3:4, :], (tiles, LANES))
        far_acc[d] = no_force
        return carry

    lax.fori_loop(0, devices, put, 0)
    mask_rows(dims, near_ref, far_q)
    for place in range(places):
        born, charge = [window_source(dims, place, halo_ref, own, 0, c) for c in range(2)]
        win_e[place, 0:1, :] = born * (1.0 / UNIT)
        win_e[place, 1:2, :] = (-0.25 * LOG2E * UNIT) / born
        win_e[place, 2:3, :] = CHARGE_UNIT * charge
        win_acc[place] = no_force
    for a in range(rows):
        for b in range(cols):
            at = slice(b, b + 1)
            for c, row in enumerate([born_ref[a, at, :], q_ref[a, at, :], r_ref[a, at, :]]):
                turned_ref[a * cols + b, c] = turned(row)

    def tile(t, carry):
        x = own_k[t]
        own_born, own_q, own_rho = [turned_ref[t, c] for c in range(3)]
        own_inv = 1.0 / own_born

        def pair(s, other_born, other_inv, charge):
            e = jnp.exp2(s * (own_inv * other_inv))
            r = lax.rsqrt(s + (own_born * other_born) * e)
            return charge * (own_q * r), (r * r) * (1.0 - 0.25 * e)

        born_near = zero
        for k in range(NEAR):
            place = window_place(t, k, cols)
            other_born, other_inv, charge = [win_e[place, c : c + 1, :] for c in range(3)]
            charge = flagged(near_ref, t, k, cols, charge)
            if k == SELF:
                charge = jnp.where(own_pair(), 0.0, charge)
            s = product(x, win_k[place])
            qr, slope = pair(s, other_born, other_inv, charge)
            f = qr * slope
            pair_f[devices + k] = f
            pair_s[devices + k] = s
            born_near = born_near + (qr - s * f)

        def far_energy(d, born_far):
            other_born, other_inv = recv_ref[d, 5:6, :], recv_ref[d, 6:7, :]
            charge = far_q[d, pl.ds(t, 1), :]
            s = product(x, far_k[d])
            qr, slope = pair(s, other_born, other_inv, charge)
            inv = 1.0 / (s + SPAN / UNIT)
            weight = s * inv
            falling = weight * slope
            pair_f[d] = qr * (falling - inv * inv)
            pair_s[d] = s
            return born_far + qr * (weight - s * falling)

        born_far = over_far(devices, far_energy, zero)
        part = own_inv * (UNIT * (0.5 * born_far + born_near))
        own_part = own_q * own_inv
        rg = jnp.sum(part, axis=1, keepdims=True) + 0.5 * (own_part * own_part)
        scale = rg * (own_rho * own_rho) * (1.0 / UNIT ** 3)

        x_twice = own_w[t]

        def force_sums(f, other_w, own_sum):
            high = f.astype(jnp.bfloat16)
            low = (f - high.astype(jnp.float32)).astype(jnp.bfloat16)
            own_sum = own_sum + product_turned(other_w, jnp.concatenate([high, low], axis=1))
            return own_sum, product(x_twice, jnp.concatenate([high, low], axis=0))

        own_sum = no_force
        for k in range(NEAR):
            place = window_place(t, k, cols)
            volume = flagged(near_ref, t, k, cols, 4.0 * win_r[place, 1:2, :])
            inv = 1.0 / (pair_s[devices + k] + win_r[place, 0:1, :])
            f = pair_f[devices + k] - (scale * volume) * (inv * inv * inv)
            if k == SELF:
                f = jnp.where(own_pair(), 0.0, f)
            own_sum, other_sum = force_sums(f, win_w[place], own_sum)
            win_acc[place] = win_acc[place] + other_sum

        def far_chain(d, own_sum):
            s = pair_s[d]
            volume = far_vol[d, pl.ds(t, 1), :]
            inv = 1.0 / (s + SPAN / UNIT)
            near = 1.0 / (s + recv_ref[d, 7:8, :])
            slope = (inv - (4.0 * s) * near) * (inv * (near * near))
            f = pair_f[d] + (scale * volume) * slope
            own_sum, other_sum = force_sums(f, far_w[d], own_sum)
            far_acc[d] = far_acc[d] + other_sum
            return own_sum

        own_sum = over_far(devices, far_chain, own_sum)
        a, b = t // cols, t % cols
        rgrad_ref[a, pl.ds(b, 1), :] = rg.T[0:1]
        total, moment = weighted(own_sum)
        grad = win_c[window_place(t, SELF, cols), 0:3, :] * total - moment
        for c in range(3):
            grad_ref[c, a, pl.ds(b, 1), :] = grad[c : c + 1]
        return carry

    lax.fori_loop(0, tiles, tile, 0)

    def send_far(d, carry):
        total, moment = weighted(far_acc[d])
        send_ref[d, 0:3, :] = far_c[d, 0:3, :] * total - moment
        return carry

    lax.fori_loop(0, devices, send_far, 0)

    def partner_grad(az, bs):
        place = (az + 1) * (cols + 2) + bs + 1
        total, moment = weighted(win_acc[place])
        return win_c[place, 0:3, :] * total - moment

    for a in range(rows):
        for b in range(cols):
            grad = partner_grad(a, b)
            for c in range(3):
                grad_ref[c, a, b : b + 1, :] = grad_ref[c, a, b : b + 1, :] + grad[c : c + 1]
    for rz in (-1, 0, 1):
        for rs in (-1, 0, 1):
            if rz == 0 and rs == 0:
                continue
            where = device_at(rz, rs, dom_count, sub_count)

            @pl.when(in_range(rz, dom_count))
            def _(rz=rz, rs=rs, where=where):
                for slot, (pa, pb) in enumerate(side_tiles(-rz, -rs, rows, cols)):
                    az = {0: pa, 1: rows, -1: -1}[rz]
                    bs = {0: pb, 1: cols, -1: -1}[rs]
                    grad = partner_grad(az, bs)
                    for c in range(3):
                        line = 3 + c * slots + slot
                        send_ref[where, line : line + 1, :] = grad[c : c + 1]


def finish_body(dims, recv_ref, grad_ref, members_ref, seg_ref, force_ref):
    rows, cols, dom_count, sub_count = dims
    slots = max(rows, cols)

    def add(d, total):
        return total + recv_ref[d, 0:3, :]

    centre_grad = lax.fori_loop(
        0, dom_count * sub_count, add, jnp.zeros((3, LANES), jnp.float32))
    per_member = centre_grad / members_ref[0:3, :]
    per_member = jnp.concatenate([per_member, jnp.zeros((5, LANES), jnp.float32)], axis=0)
    for a in range(rows):
        for b in range(cols):
            spread_out = lax.dot_general(
                per_member, member_table(seg_ref, a, b, cols), (((1,), (0,)), ((), ())),
                precision=HIGHEST, preferred_element_type=jnp.float32)
            for c in range(3):
                force_ref[c, a, b : b + 1, :] = -(
                    grad_ref[c, a, b : b + 1, :] + spread_out[c : c + 1])
    for rz in (-1, 0, 1):
        for rs in (-1, 0, 1):
            if rz == 0 and rs == 0:
                continue
            where = device_at(rz, rs, dom_count, sub_count)

            @pl.when(in_range(rz, dom_count))
            def _(rz=rz, rs=rs, where=where):
                for slot, (a, b) in enumerate(side_tiles(rz, rs, rows, cols)):
                    for c in range(3):
                        line = 3 + c * slots + slot
                        force_ref[c, a, b : b + 1, :] = (
                            force_ref[c, a, b : b + 1, :] - recv_ref[where, line : line + 1, :])


def f32(*shape):
    return jax.ShapeDtypeStruct(shape, jnp.float32)


def bf16(*shape):
    return jax.ShapeDtypeStruct(shape, jnp.bfloat16)


def local(positions, charge, radius, segment, near_tiles):
    rows, cols, width = charge.shape
    dom_count, sub_count = lax.axis_size("dom"), lax.axis_size("sub")
    dims = (rows, cols, dom_count, sub_count)
    devices = dom_count * sub_count
    tiles = rows * cols
    assert width == LANES and tiles * CT == LANES and sub_count > 2
    slots = max(rows, cols)
    places = (rows + 2) * (cols + 2)
    vmem = pltpu.MemorySpace.VMEM
    vec = (SUBLANES, LANES)

    def call(body, ins, outs, scratch=(), room=8 << 20):
        return pl.pallas_call(
            lambda *refs: body(dims, *refs),
            out_shape=outs,
            in_specs=[pl.BlockSpec(memory_space=pltpu.MemorySpace.SMEM if x is near_tiles else vmem)
                      for x in ins],
            out_specs=[pl.BlockSpec(memory_space=vmem) for _ in outs],
            scratch_shapes=list(scratch),
            compiler_params=pltpu.CompilerParams(vmem_limit_bytes=room),
            name=body.__name__,
        )(*ins)

    def exchanged(blocks):
        return lax.all_to_all(blocks, AXES, 0, 0, tiled=True)

    send, members = call(
        pack_body, (positions, charge, radius, segment),
        [f32(devices, 8 + 4 * slots, LANES), f32(*vec)])
    table = exchanged(send)
    born_radii, send, *tables = call(
        screen_body, (near_tiles, table, positions, charge, radius),
        [f32(rows, cols, LANES), f32(devices, 2 * slots, LANES),
         bf16(tiles, LANES, KROWS), bf16(tiles, WROWS, 2 * LANES),
         bf16(places, KROWS, LANES), bf16(places, WROWS, 2 * LANES),
         f32(places, *vec), f32(places, *vec),
         bf16(devices, KROWS, LANES), bf16(devices, WROWS, 2 * LANES),
         f32(devices, *vec), f32(devices, tiles, LANES)],
        room=(8 << 20) + devices * (1 << 16))
    halo = exchanged(send)
    radius_grad, grad, send = call(
        energy_body, (near_tiles, table, halo, charge, radius, born_radii, *tables),
        [f32(rows, cols, LANES), f32(3, rows, cols, LANES), f32(devices, 4 + 3 * slots, LANES)],
        [pltpu.VMEM((tiles, 3, LANES, LANES), jnp.float32),
         pltpu.VMEM((places,) + vec, jnp.float32),
         pltpu.VMEM((devices, tiles, LANES), jnp.float32),
         pltpu.VMEM((devices + NEAR, LANES, LANES), jnp.float32),
         pltpu.VMEM((devices + NEAR, LANES, LANES), jnp.float32),
         pltpu.VMEM((devices, WROWS, LANES), jnp.float32),
         pltpu.VMEM((places, WROWS, LANES), jnp.float32)],
        room=(12 << 20) + devices * (3 << 16))
    back = exchanged(send)
    forces = call(
        finish_body, (back, grad, members, segment), [f32(3, rows, cols, LANES)])[0]
    return born_radii, radius_grad, forces


def solution(mesh):
    flat = P(("groups", "dom"), "sub", None)
    stacked = P(None, ("groups", "dom"), "sub", None)
    return jax.shard_map(
        local,
        mesh=mesh,
        in_specs=(stacked, flat, flat, flat, flat),
        out_specs=(flat, flat, stacked),
        check_vma=False,
    )
```

time: 81.6 us -> 70.7 us (0.87)
  Pallas kernels: 41.3 us -> 29.7 us
    pallas_call x4, Pallas kernels: 41.3 us -> 29.7 us  [call(): pl.pallas_call(lambda *refs: body(dims, *refs), out_shape=outs, in_specs=...]
    unnamed x14 -> x20, local copies, waits for them, and re-layouts: 2.77 us -> 3.48 us
where the time goes in v2:
time: 70.7 us; the launch traced here: 70.2 us
  blocking collectives  36.4 us (51%)
  Pallas kernels  29.7 us (42%)
  local copies, waits for them, and re-layouts  3.48 us (5%)
    all_to_all x3, blocking collectives, exchanged(): return lax.all_to_all(blocks, AXES, 0, 0, tiled=True)  36.4 us
    pallas_call x4, Pallas kernels, call(): pl.pallas_call(lambda *refs: body(dims, *refs), out_shape=outs, in_specs=...  29.7 us
    unnamed x20, local copies, waits for them, and re-layouts  3.48 us

profile of v2, /device:TPU:0, one launch (start us, length us, event | category | flops | bytes accessed | tf_op | source)
XLA Modules:
  0.0 70.2 jit_solution(16775401828584357529)
XLA Ops:
  0.6 0.0 copy-start
  0.6 0.7 copy-done
  1.3 0.0 copy-start.2
  1.3 0.7 copy-done.2
  2.0 0.0 copy-start.4
  2.0 0.7 copy-done.4
  2.7 0.0 copy-start.7
  2.7 0.7 copy-done.7
  3.4 1.1 %pack_body.1 = (f32[16,24,128]{2,1,0:T(8,128)S(1)}, f32[8,128]{1,0:T(8,128)S(1)}) custom-call(f32[3,2,4,128]{3,2,1,0:T(4,128)S(1)} %copy-done, f32[2,4,128]{2,1,0:T(4,128)S(1)} %copy-done.2, f32[2,4,128]{2,1,0:T(4,128)S(1)} %copy-done.4, s32[2,4,128]{2,1,0:T(4,128)S(1)} %copy-done.7), custom_call_target="tpu_custom_call" | custom-call | tf_op jit(solution)/shard_map/pack_body/pallas_call | solution.py:510
  4.5 0.0 copy-start.1
  4.5 0.0 copy-start.3
  4.5 0.0 copy-start.5
  4.5 0.0 copy-start.6
  4.5 16.3 %all_to_all.15.refs_1_ = f32[16,24,128]{2,1,0:T(8,128)S(1)} all-to-all(f32[16,24,128]{2,1,0:T(8,128)S(1)} %get-tuple-element.20), channel_id=1, replica_groups=mesh['groups'=2,'dom'=4,'sub'=4] {'dom','sub'}, dimensions={0} | all-to-all | bytes 393216 | tf_op jit(solution)/shard_map/all_to_all | solution.py:522
  20.8 0.0 copy-done.1
  20.8 0.0 copy-done.3
  20.8 0.0 copy-done.5
  20.8 0.0 copy-done.6
  20.8 7.0 %screen_body.1 = (f32[2,4,128]{2,1,0:T(4,128)}, f32[16,8,128]{2,1,0:T(8,128)S(1)}, bf16[8,128,48]{2,1,0:T(8,128)(2,1)S(1)}, bf16[8,16,256]{2,1,0:T(8,128)(2,1)S(...) custom-call(s32[2,4,8]{2,1,0:T(4,128)S(1)} %copy-done.6, ...), custom_call_target="tpu_custom_call" | custom-call | tf_op jit(solution)/shard_map/screen_body/pallas_call | solution.py:510
  27.9 9.5 %all_to_all.16.refs_2_ = f32[16,8,128]{2,1,0:T(8,128)S(1)} all-to-all(f32[16,8,128]{2,1,0:T(8,128)S(1)} %get-tuple-element.22), channel_id=1, replica_groups=mesh['groups'=2,'dom'=4,'sub'=4] {'dom','sub'}, dimensions={0} | all-to-all | bytes 131072 | tf_op jit(solution)/shard_map/all_to_all | solution.py:522
  37.3 0.0 copy-start.9
  37.3 0.7 copy-done.9
  38.0 20.3 %energy_body.1 = (f32[2,4,128]{2,1,0:T(4,128)}, f32[3,2,4,128]{3,2,1,0:T(4,128)S(1)}, f32[16,16,128]{2,1,0:T(8,128)S(1)}) custom-call(s32[2,4,8]{2,1,0:T(4,128)S(1)} %copy-done.6, f32[16,24,128]{2,1,0:T(8,128)S(1)} %all_to_all.15.refs_1_, f32[16,8,128]{2,1,0:T(8,128)S(1)} %all_to_all.16.refs_2_, f32[2,4,128]{2,1,0:T(4,128)S(1)} %copy-done.3, ...), custom_call_target="tpu_custom_call" | custom-call | tf_op jit(solution)/shard_map/energy_body/pallas_call | solution.py:510
  58.3 0.0 copy-start.8
  58.4 10.6 %all_to_all.17.refs_0_ = f32[16,16,128]{2,1,0:T(8,128)S(1)} all-to-all(f32[16,16,128]{2,1,0:T(8,128)S(1)} %get-tuple-element.34), channel_id=1, replica_groups=mesh['groups'=2,'dom'=4,'sub'=4] {'dom','sub'}, dimensions={0} | all-to-all | bytes 262144 | tf_op jit(solution)/shard_map/all_to_all | solution.py:522
  69.0 0.0 copy-done.8
  69.0 1.2 %finish_body.1 = f32[3,2,4,128]{3,2,1,0:T(4,128)} custom-call(f32[16,16,128]{2,1,0:T(8,128)S(1)} %all_to_all.17.refs_0_, f32[3,2,4,128]{3,2,1,0:T(4,128)S(1)} %get-tuple-element.35.refs_1_, f32[8,128]{1,0:T(8,128)S(1)} %get-tuple-element.36.refs_2_, s32[2,4,128]{2,1,0:T(4,128)S(1)} %copy-done.8), custom_call_target="tpu_custom_call" | custom-call | tf_op jit(solution)/shard_map/finish_body/pallas_call | solution.py:510
Async XLA Ops:
  0.6 0.7 %copy-start = (f32[3,2,4,128]{3,2,1,0:T(4,128)S(1)}, f32[3,2,4,128]{3,2,1,0:T(4,128)}, u32[]{:S(2)}) copy-start(f32[3,2,4,128]{3,2,1,0:T(4,128)} %refs_2_.3) | copy-start | bytes 36868
  1.3 0.7 copy-start.2
  2.0 0.7 copy-start.4
  2.7 0.7 copy-start.7
  4.5 16.3 %copy-start.1 = (f32[3,2,4,128]{3,2,1,0:T(4,128)S(1)}, f32[3,2,4,128]{3,2,1,0:T(4,128)}, u32[]{:S(2)}) copy-start(f32[3,2,4,128]{3,2,1,0:T(4,128)} %refs_2_.3) | copy-start | bytes 36868
  4.5 16.3 %copy-start.3 = (f32[2,4,128]{2,1,0:T(4,128)S(1)}, f32[2,4,128]{2,1,0:T(4,128)}, u32[]{:S(2)}) copy-start(f32[2,4,128]{2,1,0:T(4,128)} %refs_3_.6) | copy-start | bytes 12292
  4.5 16.3 %copy-start.5 = (f32[2,4,128]{2,1,0:T(4,128)S(1)}, f32[2,4,128]{2,1,0:T(4,128)}, u32[]{:S(2)}) copy-start(f32[2,4,128]{2,1,0:T(4,128)} %refs_4_.3) | copy-start | bytes 12292
  4.5 16.3 %copy-start.6 = (s32[2,4,8]{2,1,0:T(4,128)S(1)}, s32[2,4,8]{2,1,0:T(4,128)}, u32[]{:S(2)}) copy-start(s32[2,4,8]{2,1,0:T(4,128)} %refs_0_.5) | copy-start | bytes 772
  37.3 0.7 copy-start.9
  58.3 10.6 %copy-start.8 = (s32[2,4,128]{2,1,0:T(4,128)S(1)}, s32[2,4,128]{2,1,0:T(4,128)}, u32[]{:S(2)}) copy-start(s32[2,4,128]{2,1,0:T(4,128)} %refs_3_.7) | copy-start | bytes 12292

commit v3 on v2

--- a/solution.py
+++ b/solution.py
@@ -9,6 +9,7 @@
 LANES = 128
 SUBLANES = 8
 UNIT = 128.0
+TOGETHER = 4
 KROWS = 48
 WROWS = 16
 SPAN = 64.0
@@ -119,8 +120,17 @@
     return jnp.sum(block.T, axis=0, keepdims=True)
 
 
-def pack_body(dims, pos_ref, q_ref, r_ref, seg_ref, send_ref, members_ref):
+def pack_body(dims, pos_hbm, q_hbm, r_hbm, seg_hbm, send_ref, members_ref,
+              pos_ref, q_ref, r_ref, seg_ref, arrived):
     rows, cols, dom_count, sub_count = dims
+    copies = [
+        pltpu.make_async_copy(source, place, arrived.at[n])
+        for n, (source, place) in enumerate(
+            [(pos_hbm, pos_ref), (q_hbm, q_ref), (r_hbm, r_ref), (seg_hbm, seg_ref)])]
+    for copy in copies:
+        copy.start()
+    for copy in copies:
+        copy.wait()
     slots = max(rows, cols)
     total = jnp.zeros((SUBLANES, LANES), jnp.float32)
     one = jnp.ones((1, LANES), jnp.float32)
@@ -162,20 +172,24 @@
                     send_ref[where, line : line + 1, :] = r_ref[a, at, :]
 
 
-def mask_rows(dims, near_ref, table_ref):
+def mask_rows(dims, near_ref, tables):
     rows, cols, dom_count, sub_count = dims
-    tile_of = lax.broadcasted_iota(jnp.int32, (1, LANES), 1) // CT
+    shape = (rows * cols, LANES)
+    row = lax.broadcasted_iota(jnp.int32, shape, 0)
+    tile_of = lax.broadcasted_iota(jnp.int32, shape, 1) // CT
+    struck = {}
     for a in range(rows):
         for b in range(cols):
-            t = a * cols + b
             for k in range(NEAR):
-                (rz, rs), _, (pa, pb) = partner(a, b, k, rows, cols)
-                where = device_at(rz, rs, dom_count, sub_count)
-                struck = tile_of == pa * cols + pb
-                if k < SELF:
-                    struck = struck & (near_ref[a, b, k] == 1)
-                kept = table_ref[where, t : t + 1, :]
-                table_ref[where, t : t + 1, :] = jnp.where(struck, 0.0, kept)
+                rel, _, (pa, pb) = partner(a, b, k, rows, cols)
+                flag = near_ref[a, b, k] if k < SELF else 1
+                at = jnp.where(row == a * cols + b, tile_of - (pa * cols + pb), 1)
+                hit = jnp.where(at == 0, flag, 0)
+                struck[rel] = struck[rel] | hit if rel in struck else hit
+    for (rz, rs), hit in struck.items():
+        where = device_at(rz, rs, dom_count, sub_count)
+        for table in tables:
+            table[where] = jnp.where(hit == 1, 0.0, table[where])
 
 
 def near_source(dims, rz, rs):
@@ -224,8 +238,8 @@
     return lax.fori_loop(0, devices // unroll, chunk, carry)
 
 
-def screen_body(dims, near_ref, recv_ref, pos_ref, q_ref, r_ref, born_ref, send_ref,
-                own_k, own_w, win_k, win_w, win_c, win_r, far_k, far_w, far_c, far_vol):
+def screen_body(dims, near_ref, recv_ref, pos_ref, q_ref, r_ref, born_out, send_ref, born_ref,
+                own_k, own_w, win_k, win_w, win_c, win_r, far_k, far_w, far_c, far_vol, far_q):
     rows, cols, dom_count, sub_count = dims
     devices = dom_count * sub_count
     slots = max(rows, cols)
@@ -242,6 +256,7 @@
         return r_ref[a, b : b + 1, :]
 
     def put(d, carry):
+        far_q[d] = jnp.broadcast_to(recv_ref[d, 3:4, :], (rows * cols, LANES))
         far_vol[d] = jnp.broadcast_to(recv_ref[d, 4:5, :], (rows * cols, LANES))
         points = jnp.where(line < 3, recv_ref[d, 0:8, :] - middle, 0.0)
         far_c[d] = points
@@ -249,7 +264,7 @@
         return carry
 
     lax.fori_loop(0, devices, put, 0)
-    mask_rows(dims, near_ref, far_vol)
+    mask_rows(dims, near_ref, (far_vol, far_q))
     none = jnp.zeros((SUBLANES - 3, LANES), jnp.float32)
     for place in range((rows + 2) * (cols + 2)):
         x, y, z, rho = [window_source(dims, place, recv_ref, own, 8, c) for c in range(4)]
@@ -262,31 +277,42 @@
         if 0 <= az < rows and 0 <= bs < cols:
             own_k[az * cols + bs], own_w[az * cols + bs] = own_tables(points)
 
-    def tile(t, carry):
-        x = own_k[t]
-        sums = jnp.zeros((LANES, LANES), jnp.float32)
-        for k in range(NEAR):
-            place = window_place(t, k, cols)
-            volume = flagged(near_ref, t, k, cols, win_r[place, 1:2, :])
-            if k == SELF:
-                volume = jnp.where(own_pair(), 0.0, volume)
-            near = product(x, win_k[place]) + win_r[place, 0:1, :]
-            sums = sums + volume / (near * near)
+    def tiles(n, carry):
+        pair = [n * TOGETHER + i for i in range(TOGETHER)]
+        x = [own_k[t] for t in pair]
+        sums = []
+        for i, t in enumerate(pair):
+            total = jnp.zeros((LANES, LANES), jnp.float32)
+            for k in range(NEAR):
+                place = window_place(t, k, cols)
+                volume = flagged(near_ref, t, k, cols, win_r[place, 1:2, :])
+                if k == SELF:
+                    volume = jnp.where(own_pair(), 0.0, volume)
+                near = product(x[i], win_k[place]) + win_r[place, 0:1, :]
+                total = total + volume / (near * near)
+            sums.append(total)
+        x_all = jnp.concatenate(x, axis=0)
 
         def far(d, sums):
-            s = product(x, far_k[d])
-            near = s + recv_ref[d, 7:8, :]
-            volume = far_vol[d, pl.ds(t, 1), :]
-            return sums + (volume * s) / ((s + SPAN / UNIT) * (near * near))
-
-        sums = over_far(devices, far, sums)
-        screening = lane_sums(sums) * (1.0 / (UNIT * UNIT))
-        a, b = t // cols, t % cols
-        rho = r_ref[a, pl.ds(b, 1), :]
-        born_ref[a, pl.ds(b, 1), :] = rho * (1.0 + rho * screening)
+            s_all = product(x_all, far_k[d])
+            out = []
+            for i, t in enumerate(pair):
+                s = s_all[i * LANES : (i + 1) * LANES]
+                near = s + recv_ref[d, 7:8, :]
+                volume = far_vol[d, pl.ds(t, 1), :]
+                out.append(sums[i] + (volume * s) / ((s + SPAN / UNIT) * (near * near)))
+            return tuple(out)
+
+        sums = over_far(devices, far, tuple(sums))
+        for i, t in enumerate(pair):
+            screening = lane_sums(sums[i]) * (1.0 / (UNIT * UNIT))
+            a, b = t // cols, t % cols
+            rho = r_ref[a, pl.ds(b, 1), :]
+            born_ref[a, pl.ds(b, 1), :] = rho * (1.0 + rho * screening)
         return carry
 
-    lax.fori_loop(0, rows * cols, tile, 0)
+    lax.fori_loop(0, rows * cols // TOGETHER, tiles, 0)
+    born_out[...] = born_ref[...]
     for rz in (-1, 0, 1):
         for rs in (-1, 0, 1):
             where = device_at(rz, rs, dom_count, sub_count)
@@ -300,10 +326,11 @@
 
 
 def energy_body(dims, near_ref, recv_ref, halo_ref, q_ref, r_ref, born_ref,
-                own_k, own_w, win_k, win_w, win_c, win_r, far_k, far_w, far_c, far_vol,
+                own_k, own_w, win_k, win_w, win_c, win_r, far_k, far_w, far_c, far_vol, far_q,
                 rgrad_ref, grad_ref, send_ref,
-                turned_ref, win_e, far_q, pair_f, pair_s, far_acc, win_acc):
+                turned_ref, win_e, pair_f, pair_s, far_acc, win_acc):
     rows, cols, dom_count, sub_count = dims
+    together = pair_f.shape[0]
     devices = dom_count * sub_count
     slots = max(rows, cols)
     tiles = rows * cols
@@ -317,12 +344,10 @@
     no_force = jnp.zeros((WROWS, LANES), jnp.float32)
 
     def put(d, carry):
-        far_q[d] = jnp.broadcast_to(recv_ref[d, 3:4, :], (tiles, LANES))
         far_acc[d] = no_force
         return carry
 
     lax.fori_loop(0, devices, put, 0)
-    mask_rows(dims, near_ref, far_q)
     for place in range(places):
         born, charge = [window_source(dims, place, halo_ref, own, 0, c) for c in range(2)]
         win_e[place, 0:1, :] = born * (1.0 / UNIT)
@@ -335,88 +360,104 @@
             for c, row in enumerate([born_ref[a, at, :], q_ref[a, at, :], r_ref[a, at, :]]):
                 turned_ref[a * cols + b, c] = turned(row)
 
-    def tile(t, carry):
-        x = own_k[t]
-        own_born, own_q, own_rho = [turned_ref[t, c] for c in range(3)]
-        own_inv = 1.0 / own_born
-
-        def pair(s, other_born, other_inv, charge):
-            e = jnp.exp2(s * (own_inv * other_inv))
+    def group(n, carry):
+        members = [n * together + i for i in range(together)]
+        own_rows = [[turned_ref[t, c] for c in range(3)] for t in members]
+        own_inv = [1.0 / rows_of[0] for rows_of in own_rows]
+
+        def pair(i, s, other_born, other_inv, charge):
+            own_born, own_q, _ = own_rows[i]
+            e = jnp.exp2(s * (own_inv[i] * other_inv))
             r = lax.rsqrt(s + (own_born * other_born) * e)
             return charge * (own_q * r), (r * r) * (1.0 - 0.25 * e)
 
-        born_near = zero
-        for k in range(NEAR):
-            place = window_place(t, k, cols)
-            other_born, other_inv, charge = [win_e[place, c : c + 1, :] for c in range(3)]
-            charge = flagged(near_ref, t, k, cols, charge)
-            if k == SELF:
-                charge = jnp.where(own_pair(), 0.0, charge)
-            s = product(x, win_k[place])
-            qr, slope = pair(s, other_born, other_inv, charge)
-            f = qr * slope
-            pair_f[devices + k] = f
-            pair_s[devices + k] = s
-            born_near = born_near + (qr - s * f)
-
+        born_near = []
+        for i, t in enumerate(members):
+            x, total = own_k[t], zero
+            for k in range(NEAR):
+                place = window_place(t, k, cols)
+                other_born, other_inv, charge = [win_e[place, c : c + 1, :] for c in range(3)]
+                charge = flagged(near_ref, t, k, cols, charge)
+                if k == SELF:
+                    charge = jnp.where(own_pair(), 0.0, charge)
+                s = product(x, win_k[place])
+                qr, slope = pair(i, s, other_born, other_inv, charge)
+                f = qr * slope
+                pair_f[i, devices + k] = f
+                pair_s[i, devices + k] = s
+                total = total + (qr - s * f)
+            born_near.append(total)
         def far_energy(d, born_far):
+            x_all = jnp.concatenate([own_k[t] for t in members], axis=0)
             other_born, other_inv = recv_ref[d, 5:6, :], recv_ref[d, 6:7, :]
-            charge = far_q[d, pl.ds(t, 1), :]
-            s = product(x, far_k[d])
-            qr, slope = pair(s, other_born, other_inv, charge)
-            inv = 1.0 / (s + SPAN / UNIT)
-            weight = s * inv
-            falling = weight * slope
-            pair_f[d] = qr * (falling - inv * inv)
-            pair_s[d] = s
-            return born_far + qr * (weight - s * falling)
-
-        born_far = over_far(devices, far_energy, zero)
-        part = own_inv * (UNIT * (0.5 * born_far + born_near))
-        own_part = own_q * own_inv
-        rg = jnp.sum(part, axis=1, keepdims=True) + 0.5 * (own_part * own_part)
-        scale = rg * (own_rho * own_rho) * (1.0 / UNIT ** 3)
-
-        x_twice = own_w[t]
-
-        def force_sums(f, other_w, own_sum):
+            s_all = product(x_all, far_k[d])
+            out = []
+            for i, t in enumerate(members):
+                charge = far_q[d, pl.ds(t, 1), :]
+                s = s_all[i * LANES : (i + 1) * LANES]
+                qr, slope = pair(i, s, other_born, other_inv, charge)
+                inv = 1.0 / (s + SPAN / UNIT)
+                weight = s * inv
+                falling = weight * slope
+                pair_f[i, d] = qr * (falling - inv * inv)
+                pair_s[i, d] = s
+                out.append(born_far[i] + qr * (weight - s * falling))
+            return tuple(out)
+
+        born_far = over_far(devices, far_energy, tuple([zero] * together))
+        scale = []
+        for i, t in enumerate(members):
+            _, own_q, own_rho = own_rows[i]
+            part = own_inv[i] * (UNIT * (0.5 * born_far[i] + born_near[i]))
+            own_part = own_q * own_inv[i]
+            rg = jnp.sum(part, axis=1, keepdims=True) + 0.5 * (own_part * own_part)
+            scale.append(rg * (own_rho * own_rho) * (1.0 / UNIT ** 3))
+            rgrad_ref[t // cols, pl.ds(t % cols, 1), :] = rg.T[0:1]
+
+        def halves(f):
             high = f.astype(jnp.bfloat16)
-            low = (f - high.astype(jnp.float32)).astype(jnp.bfloat16)
-            own_sum = own_sum + product_turned(other_w, jnp.concatenate([high, low], axis=1))
-            return own_sum, product(x_twice, jnp.concatenate([high, low], axis=0))
-
-        own_sum = no_force
-        for k in range(NEAR):
-            place = window_place(t, k, cols)
-            volume = flagged(near_ref, t, k, cols, 4.0 * win_r[place, 1:2, :])
-            inv = 1.0 / (pair_s[devices + k] + win_r[place, 0:1, :])
-            f = pair_f[devices + k] - (scale * volume) * (inv * inv * inv)
-            if k == SELF:
-                f = jnp.where(own_pair(), 0.0, f)
-            own_sum, other_sum = force_sums(f, win_w[place], own_sum)
-            win_acc[place] = win_acc[place] + other_sum
+            return high, (f - high.astype(jnp.float32)).astype(jnp.bfloat16)
+
+        own_near = []
+        for i, t in enumerate(members):
+            total = no_force
+            for k in range(NEAR):
+                place = window_place(t, k, cols)
+                volume = flagged(near_ref, t, k, cols, 4.0 * win_r[place, 1:2, :])
+                inv = 1.0 / (pair_s[i, devices + k] + win_r[place, 0:1, :])
+                f = pair_f[i, devices + k] - (scale[i] * volume) * (inv * inv * inv)
+                if k == SELF:
+                    f = jnp.where(own_pair(), 0.0, f)
+                high, low = halves(f)
+                total = total + product_turned(win_w[place], jnp.concatenate([high, low], axis=1))
+                win_acc[place] = win_acc[place] + product(
+                    own_w[t], jnp.concatenate([high, low], axis=0))
+            own_near.append(total)
+        x_sums = jnp.concatenate([own_w[t] for t in members], axis=1)
 
         def far_chain(d, own_sum):
-            s = pair_s[d]
-            volume = far_vol[d, pl.ds(t, 1), :]
-            inv = 1.0 / (s + SPAN / UNIT)
-            near = 1.0 / (s + recv_ref[d, 7:8, :])
-            slope = (inv - (4.0 * s) * near) * (inv * (near * near))
-            f = pair_f[d] + (scale * volume) * slope
-            own_sum, other_sum = force_sums(f, far_w[d], own_sum)
-            far_acc[d] = far_acc[d] + other_sum
-            return own_sum
-
-        own_sum = over_far(devices, far_chain, own_sum)
-        a, b = t // cols, t % cols
-        rgrad_ref[a, pl.ds(b, 1), :] = rg.T[0:1]
-        total, moment = weighted(own_sum)
-        grad = win_c[window_place(t, SELF, cols), 0:3, :] * total - moment
-        for c in range(3):
-            grad_ref[c, a, pl.ds(b, 1), :] = grad[c : c + 1]
+            stack, turned_stack = [], []
+            for i, t in enumerate(members):
+                s = pair_s[i, d]
+                volume = far_vol[d, pl.ds(t, 1), :]
+                inv = 1.0 / (s + SPAN / UNIT)
+                near = 1.0 / (s + recv_ref[d, 7:8, :])
+                slope = (inv - (4.0 * s) * near) * (inv * (near * near))
+                high, low = halves(pair_f[i, d] + (scale[i] * volume) * slope)
+                stack.extend([high, low])
+                turned_stack.append(jnp.concatenate([high, low], axis=1))
+            far_acc[d] = far_acc[d] + product(x_sums, jnp.concatenate(stack, axis=0))
+            return own_sum + product_turned(far_w[d], jnp.concatenate(turned_stack, axis=0))
+
+        own_sum = over_far(devices, far_chain, jnp.concatenate(own_near, axis=1))
+        for i, t in enumerate(members):
+            total, moment = weighted(own_sum[:, i * LANES : (i + 1) * LANES])
+            grad = win_c[window_place(t, SELF, cols), 0:3, :] * total - moment
+            for c in range(3):
+                grad_ref[c, t // cols, pl.ds(t % cols, 1), :] = grad[c : c + 1]
         return carry
 
-    lax.fori_loop(0, tiles, tile, 0)
+    lax.fori_loop(0, tiles // together, group, 0)
 
     def send_far(d, carry):
         total, moment = weighted(far_acc[d])
@@ -503,49 +544,53 @@
     assert width == LANES and tiles * CT == LANES and sub_count > 2
     slots = max(rows, cols)
     places = (rows + 2) * (cols + 2)
+    together = 2 if devices <= 64 else 1
     vmem = pltpu.MemorySpace.VMEM
     vec = (SUBLANES, LANES)
 
-    def call(body, ins, outs, scratch=(), room=8 << 20):
+    def call(body, ins, outs, scratch=(), room=8 << 20, space=vmem):
         return pl.pallas_call(
             lambda *refs: body(dims, *refs),
             out_shape=outs,
-            in_specs=[pl.BlockSpec(memory_space=pltpu.MemorySpace.SMEM if x is near_tiles else vmem)
+            in_specs=[pl.BlockSpec(memory_space=pltpu.MemorySpace.SMEM if x is near_tiles else space)
                       for x in ins],
             out_specs=[pl.BlockSpec(memory_space=vmem) for _ in outs],
             scratch_shapes=list(scratch),
             compiler_params=pltpu.CompilerParams(vmem_limit_bytes=room),
             name=body.__name__,
-        )(*ins)
+        )(*[pltpu.with_memory_space_constraint(x, space) if space is not vmem else x for x in ins])
 
     def exchanged(blocks):
         return lax.all_to_all(blocks, AXES, 0, 0, tiled=True)
 
     send, members = call(
         pack_body, (positions, charge, radius, segment),
-        [f32(devices, 8 + 4 * slots, LANES), f32(*vec)])
+        [f32(devices, 8 + 4 * slots, LANES), f32(*vec)],
+        [pltpu.VMEM(positions.shape, jnp.float32), pltpu.VMEM(charge.shape, jnp.float32),
+         pltpu.VMEM(radius.shape, jnp.float32), pltpu.VMEM(segment.shape, jnp.int32),
+         pltpu.SemaphoreType.DMA((4,))],
+        space=pltpu.MemorySpace.HBM)
     table = exchanged(send)
     born_radii, send, *tables = call(
         screen_body, (near_tiles, table, positions, charge, radius),
-        [f32(rows, cols, LANES), f32(devices, 2 * slots, LANES),
+        [f32(rows, cols, LANES), f32(devices, 2 * slots, LANES), f32(rows, cols, LANES),
          bf16(tiles, LANES, KROWS), bf16(tiles, WROWS, 2 * LANES),
          bf16(places, KROWS, LANES), bf16(places, WROWS, 2 * LANES),
          f32(places, *vec), f32(places, *vec),
          bf16(devices, KROWS, LANES), bf16(devices, WROWS, 2 * LANES),
-         f32(devices, *vec), f32(devices, tiles, LANES)],
+         f32(devices, *vec), f32(devices, tiles, LANES), f32(devices, tiles, LANES)],
         room=(8 << 20) + devices * (1 << 16))
     halo = exchanged(send)
     radius_grad, grad, send = call(
-        energy_body, (near_tiles, table, halo, charge, radius, born_radii, *tables),
+        energy_body, (near_tiles, table, halo, charge, radius, *tables),
         [f32(rows, cols, LANES), f32(3, rows, cols, LANES), f32(devices, 4 + 3 * slots, LANES)],
         [pltpu.VMEM((tiles, 3, LANES, LANES), jnp.float32),
          pltpu.VMEM((places,) + vec, jnp.float32),
-         pltpu.VMEM((devices, tiles, LANES), jnp.float32),
-         pltpu.VMEM((devices + NEAR, LANES, LANES), jnp.float32),
-         pltpu.VMEM((devices + NEAR, LANES, LANES), jnp.float32),
+         pltpu.VMEM((together, devices + NEAR, LANES, LANES), jnp.float32),
+         pltpu.VMEM((together, devices + NEAR, LANES, LANES), jnp.float32),
          pltpu.VMEM((devices, WROWS, LANES), jnp.float32),
          pltpu.VMEM((places, WROWS, LANES), jnp.float32)],
-        room=(12 << 20) + devices * (3 << 16))
+        room=(12 << 20) + together * devices * (3 << 16))
     back = exchanged(send)
     forces = call(
         finish_body, (back, grad, members, segment), [f32(3, rows, cols, LANES)])[0]

time: 70.7 us -> 65.3 us (0.924)
  local copies, waits for them, and re-layouts: 3.48 us -> 0.03 us
  Pallas kernels: 29.7 us -> 27.8 us
    unnamed x20 -> x10, local copies, waits for them, and re-layouts: 3.48 us -> 0.03 us
    pallas_call x4, Pallas kernels: 29.7 us -> 27.8 us  [call(): pl.pallas_call(lambda *refs: body(dims, *refs), out_shape=outs, in_specs=...]
where the time goes in v3:
time: 65.3 us; the launch traced here: 64.9 us
  blocking collectives  36.4 us (56%)
  Pallas kernels  27.8 us (43%)
  between operations  0.68 us (1%)
    all_to_all x3, blocking collectives, exchanged(): return lax.all_to_all(blocks, AXES, 0, 0, tiled=True)  36.4 us
    pallas_call x4, Pallas kernels, call(): pl.pallas_call(lambda *refs: body(dims, *refs), out_shape=outs, in_specs=...  27.8 us

profile of v3, /device:TPU:0, one launch (start us, length us, event | category | flops | bytes accessed | tf_op | source)
XLA Modules:
  0.0 64.9 jit_solution(14234373634144759405)
XLA Ops:
  0.6 1.8 %pack_body.1 = (f32[16,24,128]{2,1,0:T(8,128)S(1)}, f32[8,128]{1,0:T(8,128)S(1)}) custom-call(f32[3,2,4,128]{3,2,1,0:T(4,128)} %refs_2_.3, f32[2,4,128]{2,1,0:T(4,128)} %refs_3_.6, f32[2,4,128]{2,1,0:T(4,128)} %refs_4_.3, s32[2,4,128]{2,1,0:T(4,128)} %refs_3_.7), custom_call_target="tpu_custom_call" | custom-call | tf_op jit(solution)/shard_map/pack_body/pallas_call | solution.py:552
  2.5 0.0 copy-start
  2.5 0.0 copy-start.1
  2.5 0.0 copy-start.2
  2.5 0.0 copy-start.3
  2.5 16.3 %all_to_all.15.refs_1_ = f32[16,24,128]{2,1,0:T(8,128)S(1)} all-to-all(f32[16,24,128]{2,1,0:T(8,128)S(1)} %get-tuple-element.22), channel_id=1, replica_groups=mesh['groups'=2,'dom'=4,'sub'=4] {'dom','sub'}, dimensions={0} | all-to-all | bytes 393216 | tf_op jit(solution)/shard_map/all_to_all | solution.py:564
  18.8 0.0 copy-done
  18.8 0.0 copy-done.1
  18.8 0.0 copy-done.2
  18.8 0.0 copy-done.3
  18.8 5.8 %screen_body.1 = (f32[2,4,128]{2,1,0:T(4,128)}, f32[16,8,128]{2,1,0:T(8,128)S(1)}, f32[2,4,128]{2,1,0:T(4,128)S(1)}, bf16[8,128,48]{2,1,0:T(8,128)(2,1)S(1)}, bf...) custom-call(s32[2,4,8]{2,1,0:T(4,128)S(1)} %copy-done.3, ...), custom_call_target="tpu_custom_call" | custom-call | tf_op jit(solution)/shard_map/screen_body/pallas_call | solution.py:552
  24.6 9.5 %all_to_all.16.refs_2_ = f32[16,8,128]{2,1,0:T(8,128)S(1)} all-to-all(f32[16,8,128]{2,1,0:T(8,128)S(1)} %get-tuple-element.24), channel_id=1, replica_groups=mesh['groups'=2,'dom'=4,'sub'=4] {'dom','sub'}, dimensions={0} | all-to-all | bytes 131072 | tf_op jit(solution)/shard_map/all_to_all | solution.py:564
  34.1 18.9 %energy_body.1 = (f32[2,4,128]{2,1,0:T(4,128)}, f32[3,2,4,128]{3,2,1,0:T(4,128)S(1)}, f32[16,16,128]{2,1,0:T(8,128)S(1)}) custom-call(s32[2,4,8]{2,1,0:T(4,128)S(1)} %copy-done.3, f32[16,24,128]{2,1,0:T(8,128)S(1)} %all_to_all.15.refs_1_, f32[16,8,128]{2,1,0:T(8,128)S(1)} %all_to_all.16.refs_2_, f32[2,4,128]{2,1,0:T(4,128)S(1)} %copy-done.1, ...), custom_call_target="tpu_custom_call" | custom-call | tf_op jit(solution)/shard_map/energy_body/pallas_call | solution.py:552
  53.0 0.0 copy-start.4
  53.0 10.6 %all_to_all.17.refs_0_ = f32[16,16,128]{2,1,0:T(8,128)S(1)} all-to-all(f32[16,16,128]{2,1,0:T(8,128)S(1)} %get-tuple-element.38), channel_id=1, replica_groups=mesh['groups'=2,'dom'=4,'sub'=4] {'dom','sub'}, dimensions={0} | all-to-all | bytes 262144 | tf_op jit(solution)/shard_map/all_to_all | solution.py:564
  63.7 0.0 copy-done.4
  63.7 1.2 %finish_body.1 = f32[3,2,4,128]{3,2,1,0:T(4,128)} custom-call(f32[16,16,128]{2,1,0:T(8,128)S(1)} %all_to_all.17.refs_0_, f32[3,2,4,128]{3,2,1,0:T(4,128)S(1)} %get-tuple-element.39.refs_1_, f32[8,128]{1,0:T(8,128)S(1)} %get-tuple-element.40.refs_2_, s32[2,4,128]{2,1,0:T(4,128)S(1)} %copy-done.4), custom_call_target="tpu_custom_call" | custom-call | tf_op jit(solution)/shard_map/finish_body/pallas_call | solution.py:552
Async XLA Ops:
  2.5 16.3 %copy-start = (f32[3,2,4,128]{3,2,1,0:T(4,128)S(1)}, f32[3,2,4,128]{3,2,1,0:T(4,128)}, u32[]{:S(2)}) copy-start(f32[3,2,4,128]{3,2,1,0:T(4,128)} %refs_2_.3) | copy-start | bytes 36868
  2.5 16.3 %copy-start.1 = (f32[2,4,128]{2,1,0:T(4,128)S(1)}, f32[2,4,128]{2,1,0:T(4,128)}, u32[]{:S(2)}) copy-start(f32[2,4,128]{2,1,0:T(4,128)} %refs_3_.6) | copy-start | bytes 12292
  2.5 16.3 %copy-start.2 = (f32[2,4,128]{2,1,0:T(4,128)S(1)}, f32[2,4,128]{2,1,0:T(4,128)}, u32[]{:S(2)}) copy-start(f32[2,4,128]{2,1,0:T(4,128)} %refs_4_.3) | copy-start | bytes 12292
  2.5 16.3 %copy-start.3 = (s32[2,4,8]{2,1,0:T(4,128)S(1)}, s32[2,4,8]{2,1,0:T(4,128)}, u32[]{:S(2)}) copy-start(s32[2,4,8]{2,1,0:T(4,128)} %refs_0_.5) | copy-start | bytes 772
  53.0 10.6 %copy-start.4 = (s32[2,4,128]{2,1,0:T(4,128)S(1)}, s32[2,4,128]{2,1,0:T(4,128)}, u32[]{:S(2)}) copy-start(s32[2,4,128]{2,1,0:T(4,128)} %refs_3_.7) | copy-start | bytes 12292

commit v4 on v3

--- a/solution.py
+++ b/solution.py
@@ -109,7 +109,7 @@
 def member_table(seg_ref, a, b, cols):
     comp = lax.broadcasted_iota(jnp.int32, (LANES, LANES), 0)
     owner = seg_ref[a, b : b + 1, :] + (a * cols + b) * CT
-    return (comp == owner).astype(jnp.float32)
+    return (comp == owner).astype(jnp.float32).astype(jnp.bfloat16)
 
 
 def turned(row):
@@ -120,7 +120,7 @@
     return jnp.sum(block.T, axis=0, keepdims=True)
 
 
-def pack_body(dims, pos_hbm, q_hbm, r_hbm, seg_hbm, send_ref, members_ref,
+def pack_body(dims, pos_hbm, q_hbm, r_hbm, seg_hbm, send_ref, members_ref, member_ref,
               pos_ref, q_ref, r_ref, seg_ref, arrived):
     rows, cols, dom_count, sub_count = dims
     copies = [
@@ -132,18 +132,19 @@
     for copy in copies:
         copy.wait()
     slots = max(rows, cols)
-    total = jnp.zeros((SUBLANES, LANES), jnp.float32)
     one = jnp.ones((1, LANES), jnp.float32)
+    values = []
     for a in range(rows):
         for b in range(cols):
-            at = slice(b, b + 1)
+            at, t = slice(b, b + 1), a * cols + b
             rho = r_ref[a, at, :]
-            values = jnp.concatenate(
+            member_ref[:, t * LANES : (t + 1) * LANES] = member_table(seg_ref, a, b, cols)
+            block = pieces(jnp.concatenate(
                 [pos_ref[0, a, at, :], pos_ref[1, a, at, :], pos_ref[2, a, at, :],
-                 q_ref[a, at, :], rho * rho * rho, rho, one, one], axis=0)
-            total = total + lax.dot_general(
-                values, member_table(seg_ref, a, b, cols), (((1,), (1,)), ((), ())),
-                precision=HIGHEST, preferred_element_type=jnp.float32)
+                 q_ref[a, at, :], rho * rho * rho, rho, one, one], axis=0))
+            values.append(jnp.concatenate(block + (jnp.zeros_like(block[0]),), axis=0))
+    sums = product_turned(jnp.concatenate(values, axis=1).astype(jnp.bfloat16), member_ref[...])
+    total = sums[0:8] + sums[8:16] + sums[16:24]
     members = total[6:7]
     comp_radius = RADIUS_FACTOR * total[5:6] / members
     table = jnp.concatenate(
@@ -238,7 +239,7 @@
     return lax.fori_loop(0, devices // unroll, chunk, carry)
 
 
-def screen_body(dims, near_ref, recv_ref, pos_ref, q_ref, r_ref, born_out, send_ref, born_ref,
+def screen_body(dims, near_ref, recv_ref, pos_ref, q_ref, r_ref, send_ref, born_ref,
                 own_k, own_w, win_k, win_w, win_c, win_r, far_k, far_w, far_c, far_vol, far_q):
     rows, cols, dom_count, sub_count = dims
     devices = dom_count * sub_count
@@ -312,7 +313,6 @@
         return carry
 
     lax.fori_loop(0, rows * cols // TOGETHER, tiles, 0)
-    born_out[...] = born_ref[...]
     for rz in (-1, 0, 1):
         for rs in (-1, 0, 1):
             where = device_at(rz, rs, dom_count, sub_count)
@@ -493,7 +493,8 @@
                         send_ref[where, line : line + 1, :] = grad[c : c + 1]
 
 
-def finish_body(dims, recv_ref, grad_ref, members_ref, seg_ref, force_ref):
+def finish_body(dims, recv_ref, grad_ref, members_ref, member_ref, born_ref, rgrad_ref,
+                force_ref, born_out, rgrad_out):
     rows, cols, dom_count, sub_count = dims
     slots = max(rows, cols)
 
@@ -503,12 +504,16 @@
     centre_grad = lax.fori_loop(
         0, dom_count * sub_count, add, jnp.zeros((3, LANES), jnp.float32))
     per_member = centre_grad / members_ref[0:3, :]
-    per_member = jnp.concatenate([per_member, jnp.zeros((5, LANES), jnp.float32)], axis=0)
+    born_out[...] = born_ref[...]
+    rgrad_out[...] = rgrad_ref[...]
+    block = pieces(jnp.concatenate([per_member, jnp.zeros((5, LANES), jnp.float32)], axis=0))
+    block = jnp.concatenate(block + (jnp.zeros_like(block[0]),), axis=0).astype(jnp.bfloat16)
+    back = product(block, member_ref[...])
+    back = back[0:8] + back[8:16] + back[16:24]
     for a in range(rows):
         for b in range(cols):
-            spread_out = lax.dot_general(
-                per_member, member_table(seg_ref, a, b, cols), (((1,), (0,)), ((), ())),
-                precision=HIGHEST, preferred_element_type=jnp.float32)
+            t = a * cols + b
+            spread_out = back[:, t * LANES : (t + 1) * LANES]
             for c in range(3):
                 force_ref[c, a, b : b + 1, :] = -(
                     grad_ref[c, a, b : b + 1, :] + spread_out[c : c + 1])
@@ -563,17 +568,17 @@
     def exchanged(blocks):
         return lax.all_to_all(blocks, AXES, 0, 0, tiled=True)
 
-    send, members = call(
+    send, members, member = call(
         pack_body, (positions, charge, radius, segment),
-        [f32(devices, 8 + 4 * slots, LANES), f32(*vec)],
+        [f32(devices, 8 + 4 * slots, LANES), f32(*vec), bf16(LANES, tiles * LANES)],
         [pltpu.VMEM(positions.shape, jnp.float32), pltpu.VMEM(charge.shape, jnp.float32),
          pltpu.VMEM(radius.shape, jnp.float32), pltpu.VMEM(segment.shape, jnp.int32),
          pltpu.SemaphoreType.DMA((4,))],
         space=pltpu.MemorySpace.HBM)
     table = exchanged(send)
-    born_radii, send, *tables = call(
+    send, born, *tables = call(
         screen_body, (near_tiles, table, positions, charge, radius),
-        [f32(rows, cols, LANES), f32(devices, 2 * slots, LANES), f32(rows, cols, LANES),
+        [f32(devices, 2 * slots, LANES), f32(rows, cols, LANES),
          bf16(tiles, LANES, KROWS), bf16(tiles, WROWS, 2 * LANES),
          bf16(places, KROWS, LANES), bf16(places, WROWS, 2 * LANES),
          f32(places, *vec), f32(places, *vec),
@@ -582,7 +587,7 @@
         room=(8 << 20) + devices * (1 << 16))
     halo = exchanged(send)
     radius_grad, grad, send = call(
-        energy_body, (near_tiles, table, halo, charge, radius, *tables),
+        energy_body, (near_tiles, table, halo, charge, radius, born, *tables),
         [f32(rows, cols, LANES), f32(3, rows, cols, LANES), f32(devices, 4 + 3 * slots, LANES)],
         [pltpu.VMEM((tiles, 3, LANES, LANES), jnp.float32),
          pltpu.VMEM((places,) + vec, jnp.float32),
@@ -592,8 +597,10 @@
          pltpu.VMEM((places, WROWS, LANES), jnp.float32)],
         room=(12 << 20) + together * devices * (3 << 16))
     back = exchanged(send)
-    forces = call(
-        finish_body, (back, grad, members, segment), [f32(3, rows, cols, LANES)])[0]
+    shape = f32(rows, cols, LANES)
+    forces, born_radii, radius_grad = call(
+        finish_body, (back, grad, members, member, born, radius_grad),
+        [f32(3, rows, cols, LANES), shape, shape])
     return born_radii, radius_grad, forces
 
 

time: 65.3 us -> 62.8 us (0.962)
  Pallas kernels: 27.8 us -> 25.5 us
    pallas_call x4, Pallas kernels: 27.8 us -> 25.5 us  [call(): pl.pallas_call(lambda *refs: body(dims, *refs), out_shape=outs, in_specs=...]
where the time goes in v4:
time: 62.8 us; the launch traced here: 62.5 us
  blocking collectives  36.3 us (58%)
  Pallas kernels  25.5 us (41%)
  between operations  0.7 us (1%)
    all_to_all x3, blocking collectives, exchanged(): return lax.all_to_all(blocks, AXES, 0, 0, tiled=True)  36.3 us
    pallas_call x4, Pallas kernels, call(): pl.pallas_call(lambda *refs: body(dims, *refs), out_shape=outs, in_specs=...  25.5 us

profile of v4, /device:TPU:0, one launch (start us, length us, event | category | flops | bytes accessed | tf_op | source)
XLA Modules:
  0.0 62.5 jit_solution(10827202616260851317)
XLA Ops:
  0.6 1.2 %pack_body.1 = (f32[16,24,128]{2,1,0:T(8,128)S(1)}, f32[8,128]{1,0:T(8,128)S(1)}, bf16[128,1024]{1,0:T(8,128)(2,1)S(1)}) custom-call(f32[3,2,4,128]{3,2,1,0:T(4,128)} %refs_2_.3, f32[2,4,128]{2,1,0:T(4,128)} %refs_3_.5, f32[2,4,128]{2,1,0:T(4,128)} %refs_4_.3, s32[2,4,128]{2,1,0:T(4,128)} %refs_3_.3), custom_call_target="tpu_custom_call" | custom-call | tf_op jit(solution)/shard_map/pack_body/pallas_call | solution.py:557
  1.8 0.0 copy-start
  1.8 0.0 copy-start.1
  1.8 0.0 copy-start.2
  1.8 0.0 copy-start.3
  1.8 16.3 %all_to_all.15.refs_1_ = f32[16,24,128]{2,1,0:T(8,128)S(1)} all-to-all(f32[16,24,128]{2,1,0:T(8,128)S(1)} %get-tuple-element.25), channel_id=1, replica_groups=mesh['groups'=2,'dom'=4,'sub'=4] {'dom','sub'}, dimensions={0} | all-to-all | bytes 393216 | tf_op jit(solution)/shard_map/all_to_all | solution.py:569
  18.1 0.0 copy-done
  18.1 0.0 copy-done.1
  18.1 0.0 copy-done.2
  18.1 0.0 copy-done.3
  18.2 5.1 %screen_body.1 = (f32[16,8,128]{2,1,0:T(8,128)S(1)}, f32[2,4,128]{2,1,0:T(4,128)S(1)}, bf16[8,128,48]{2,1,0:T(8,128)(2,1)S(1)}, bf16[8,16,256]{2,1,0:T(8,128)(2,...) custom-call(s32[2,4,8]{2,1,0:T(4,128)S(1)} %copy-done.3, ...), custom_call_target="tpu_custom_call" | custom-call | tf_op jit(solution)/shard_map/screen_body/pallas_call | solution.py:557
  23.3 9.5 %all_to_all.16.refs_2_ = f32[16,8,128]{2,1,0:T(8,128)S(1)} all-to-all(f32[16,8,128]{2,1,0:T(8,128)S(1)} %get-tuple-element.26), channel_id=1, replica_groups=mesh['groups'=2,'dom'=4,'sub'=4] {'dom','sub'}, dimensions={0} | all-to-all | bytes 131072 | tf_op jit(solution)/shard_map/all_to_all | solution.py:569
  32.8 18.3 %energy_body.1 = (f32[2,4,128]{2,1,0:T(4,128)S(1)}, f32[3,2,4,128]{3,2,1,0:T(4,128)S(1)}, f32[16,16,128]{2,1,0:T(8,128)S(1)}) custom-call(s32[2,4,8]{2,1,0:T(4,128)S(1)} %copy-done.3, f32[16,24,128]{2,1,0:T(8,128)S(1)} %all_to_all.15.refs_1_, f32[16,8,128]{2,1,0:T(8,128)S(1)} %all_to_all.16.refs_2_, f32[2,4,128]{2,1,0:T(4,128)S(1)} %copy-done.1, ...), custom_call_target="tpu_custom_call" | custom-call | tf_op jit(solution)/shard_map/energy_body/pallas_call | solution.py:557
  51.1 10.5 %all_to_all.17.refs_0_ = f32[16,16,128]{2,1,0:T(8,128)S(1)} all-to-all(f32[16,16,128]{2,1,0:T(8,128)S(1)} %get-tuple-element.39), channel_id=1, replica_groups=mesh['groups'=2,'dom'=4,'sub'=4] {'dom','sub'}, dimensions={0} | all-to-all | bytes 262144 | tf_op jit(solution)/shard_map/all_to_all | solution.py:569
  61.6 0.9 %finish_body.1 = (f32[3,2,4,128]{3,2,1,0:T(4,128)}, f32[2,4,128]{2,1,0:T(4,128)}, f32[2,4,128]{2,1,0:T(4,128)}) custom-call(f32[16,16,128]{2,1,0:T(8,128)S(1)} %all_to_all.17.refs_0_, f32[3,2,4,128]{3,2,1,0:T(4,128)S(1)} %get-tuple-element.40.refs_1_, f32[8,128]{1,0:T(8,128)S(1)} %get-tuple-element.41.refs_2_, ...), custom_call_target="tpu_custom_call" | custom-call | tf_op jit(solution)/shard_map/finish_body/pallas_call | solution.py:557
Async XLA Ops:
  1.8 16.3 %copy-start = (f32[3,2,4,128]{3,2,1,0:T(4,128)S(1)}, f32[3,2,4,128]{3,2,1,0:T(4,128)}, u32[]{:S(2)}) copy-start(f32[3,2,4,128]{3,2,1,0:T(4,128)} %refs_2_.3) | copy-start | bytes 36868
  1.8 16.3 %copy-start.1 = (f32[2,4,128]{2,1,0:T(4,128)S(1)}, f32[2,4,128]{2,1,0:T(4,128)}, u32[]{:S(2)}) copy-start(f32[2,4,128]{2,1,0:T(4,128)} %refs_3_.5) | copy-start | bytes 12292
  1.8 16.3 %copy-start.2 = (f32[2,4,128]{2,1,0:T(4,128)S(1)}, f32[2,4,128]{2,1,0:T(4,128)}, u32[]{:S(2)}) copy-start(f32[2,4,128]{2,1,0:T(4,128)} %refs_4_.3) | copy-start | bytes 12292
  1.8 16.3 %copy-start.3 = (s32[2,4,8]{2,1,0:T(4,128)S(1)}, s32[2,4,8]{2,1,0:T(4,128)}, u32[]{:S(2)}) copy-start(s32[2,4,8]{2,1,0:T(4,128)} %refs_0_.5) | copy-start | bytes 772

commit v5 on v4

--- a/solution.py
+++ b/solution.py
@@ -52,8 +52,8 @@
     return (at >= 0) & (at < dom_count)
 
 
-def far_unroll(devices):
-    return 16 if devices % 16 == 0 else 1
+def far_unroll(pairs):
+    return 8 if pairs % 8 == 0 else 1
 
 
 def pieces(value):
@@ -226,17 +226,24 @@
     return lax.broadcasted_iota(jnp.int32, shape, 0) == lax.broadcasted_iota(jnp.int32, shape, 1)
 
 
-def over_far(devices, step, carry):
-    unroll = far_unroll(devices)
+def quarter_of(block, i, half):
+    return block[i * LANES : (i + 1) * LANES, half * LANES : (half + 1) * LANES]
+
+
+def over_far(pairs, begin, end, carry):
+    unroll = far_unroll(pairs)
 
     def chunk(n, carry):
+        begun = begin(n * unroll)
         for j in range(unroll):
-            carry = step(n * unroll + j, carry)
+            ahead = begin(n * unroll + j + 1) if j + 1 < unroll else None
+            carry = end(n * unroll + j, begun, carry)
+            begun = ahead
         return carry
 
-    if devices == unroll:
+    if pairs == unroll:
         return chunk(0, carry)
-    return lax.fori_loop(0, devices // unroll, chunk, carry)
+    return lax.fori_loop(0, pairs // unroll, chunk, carry)
 
 
 def screen_body(dims, near_ref, recv_ref, pos_ref, q_ref, r_ref, send_ref, born_ref,
@@ -256,15 +263,19 @@
             return pos_ref[c, a, b : b + 1, :]
         return r_ref[a, b : b + 1, :]
 
-    def put(d, carry):
-        far_q[d] = jnp.broadcast_to(recv_ref[d, 3:4, :], (rows * cols, LANES))
-        far_vol[d] = jnp.broadcast_to(recv_ref[d, 4:5, :], (rows * cols, LANES))
-        points = jnp.where(line < 3, recv_ref[d, 0:8, :] - middle, 0.0)
-        far_c[d] = points
-        far_k[d], far_w[d] = other_tables(points)
+    def put(p, carry):
+        for half in range(2):
+            d = 2 * p + half
+            far_q[d] = jnp.broadcast_to(recv_ref[d, 3:4, :], (rows * cols, LANES))
+            far_vol[d] = jnp.broadcast_to(recv_ref[d, 4:5, :], (rows * cols, LANES))
+            points = jnp.where(line < 3, recv_ref[d, 0:8, :] - middle, 0.0)
+            far_c[d] = points
+            table, weights = other_tables(points)
+            far_k[p, :, half * LANES : (half + 1) * LANES] = table
+            far_w[p, :, 2 * half * LANES : 2 * (half + 1) * LANES] = weights
         return carry
 
-    lax.fori_loop(0, devices, put, 0)
+    lax.fori_loop(0, devices // 2, put, 0)
     mask_rows(dims, near_ref, (far_vol, far_q))
     none = jnp.zeros((SUBLANES - 3, LANES), jnp.float32)
     for place in range((rows + 2) * (cols + 2)):
@@ -294,17 +305,21 @@
             sums.append(total)
         x_all = jnp.concatenate(x, axis=0)
 
-        def far(d, sums):
-            s_all = product(x_all, far_k[d])
-            out = []
-            for i, t in enumerate(pair):
-                s = s_all[i * LANES : (i + 1) * LANES]
-                near = s + recv_ref[d, 7:8, :]
-                volume = far_vol[d, pl.ds(t, 1), :]
-                out.append(sums[i] + (volume * s) / ((s + SPAN / UNIT) * (near * near)))
+        def far_square(p):
+            return product(x_all, far_k[p])
+
+        def far(p, s_all, sums):
+            out = list(sums)
+            for half in range(2):
+                d = 2 * p + half
+                for i, t in enumerate(pair):
+                    s = quarter_of(s_all, i, half)
+                    near = s + recv_ref[d, 7:8, :]
+                    volume = far_vol[d, pl.ds(t, 1), :]
+                    out[i] = out[i] + (volume * s) / ((s + SPAN / UNIT) * (near * near))
             return tuple(out)
 
-        sums = over_far(devices, far, tuple(sums))
+        sums = over_far(devices // 2, far_square, far, tuple(sums))
         for i, t in enumerate(pair):
             screening = lane_sums(sums[i]) * (1.0 / (UNIT * UNIT))
             a, b = t // cols, t % cols
@@ -328,9 +343,10 @@
 def energy_body(dims, near_ref, recv_ref, halo_ref, q_ref, r_ref, born_ref,
                 own_k, own_w, win_k, win_w, win_c, win_r, far_k, far_w, far_c, far_vol, far_q,
                 rgrad_ref, grad_ref, send_ref,
-                turned_ref, win_e, pair_f, pair_s, far_acc, win_acc):
+                turned_ref, win_e, pair_f, pair_s, pair_i, pair_w, far_acc, win_acc):
     rows, cols, dom_count, sub_count = dims
     together = pair_f.shape[0]
+    kept = pair_i.shape[1] == dom_count * sub_count
     devices = dom_count * sub_count
     slots = max(rows, cols)
     tiles = rows * cols
@@ -343,11 +359,11 @@
     zero = jnp.zeros((LANES, LANES), jnp.float32)
     no_force = jnp.zeros((WROWS, LANES), jnp.float32)
 
-    def put(d, carry):
-        far_acc[d] = no_force
+    def put(p, carry):
+        far_acc[p] = jnp.zeros((WROWS, 2 * LANES), jnp.float32)
         return carry
 
-    lax.fori_loop(0, devices, put, 0)
+    lax.fori_loop(0, devices // 2, put, 0)
     for place in range(places):
         born, charge = [window_source(dims, place, halo_ref, own, 0, c) for c in range(2)]
         win_e[place, 0:1, :] = born * (1.0 / UNIT)
@@ -387,24 +403,31 @@
                 pair_s[i, devices + k] = s
                 total = total + (qr - s * f)
             born_near.append(total)
-        def far_energy(d, born_far):
-            x_all = jnp.concatenate([own_k[t] for t in members], axis=0)
-            other_born, other_inv = recv_ref[d, 5:6, :], recv_ref[d, 6:7, :]
-            s_all = product(x_all, far_k[d])
-            out = []
-            for i, t in enumerate(members):
-                charge = far_q[d, pl.ds(t, 1), :]
-                s = s_all[i * LANES : (i + 1) * LANES]
-                qr, slope = pair(i, s, other_born, other_inv, charge)
-                inv = 1.0 / (s + SPAN / UNIT)
-                weight = s * inv
-                falling = weight * slope
-                pair_f[i, d] = qr * (falling - inv * inv)
-                pair_s[i, d] = s
-                out.append(born_far[i] + qr * (weight - s * falling))
+        def far_square(p):
+            return product(jnp.concatenate([own_k[t] for t in members], axis=0), far_k[p])
+
+        def far_energy(p, s_all, born_far):
+            out = list(born_far)
+            for half in range(2):
+                d = 2 * p + half
+                other_born, other_inv = recv_ref[d, 5:6, :], recv_ref[d, 6:7, :]
+                for i, t in enumerate(members):
+                    charge = far_q[d, pl.ds(t, 1), :]
+                    s = quarter_of(s_all, i, half)
+                    qr, slope = pair(i, s, other_born, other_inv, charge)
+                    inv = 1.0 / (s + SPAN / UNIT)
+                    weight = s * inv
+                    falling = weight * slope
+                    square = inv * inv
+                    pair_f[i, d] = qr * (falling - square)
+                    pair_s[i, d] = s
+                    if kept:
+                        pair_i[i, d] = square
+                        pair_w[i, d] = weight
+                    out[i] = out[i] + qr * (weight - s * falling)
             return tuple(out)
 
-        born_far = over_far(devices, far_energy, tuple([zero] * together))
+        born_far = over_far(devices // 2, far_square, far_energy, tuple([zero] * together))
         scale = []
         for i, t in enumerate(members):
             _, own_q, own_rho = own_rows[i]
@@ -435,21 +458,31 @@
             own_near.append(total)
         x_sums = jnp.concatenate([own_w[t] for t in members], axis=1)
 
-        def far_chain(d, own_sum):
-            stack, turned_stack = [], []
-            for i, t in enumerate(members):
-                s = pair_s[i, d]
-                volume = far_vol[d, pl.ds(t, 1), :]
-                inv = 1.0 / (s + SPAN / UNIT)
-                near = 1.0 / (s + recv_ref[d, 7:8, :])
-                slope = (inv - (4.0 * s) * near) * (inv * (near * near))
-                high, low = halves(pair_f[i, d] + (scale[i] * volume) * slope)
-                stack.extend([high, low])
-                turned_stack.append(jnp.concatenate([high, low], axis=1))
-            far_acc[d] = far_acc[d] + product(x_sums, jnp.concatenate(stack, axis=0))
-            return own_sum + product_turned(far_w[d], jnp.concatenate(turned_stack, axis=0))
-
-        own_sum = over_far(devices, far_chain, jnp.concatenate(own_near, axis=1))
+        def far_factors(p):
+            parts = [[], []]
+            for half in range(2):
+                d = 2 * p + half
+                for i, t in enumerate(members):
+                    s = pair_s[i, d]
+                    volume = far_vol[d, pl.ds(t, 1), :]
+                    near = 1.0 / (s + recv_ref[d, 7:8, :])
+                    if kept:
+                        square, weight = pair_i[i, d], pair_w[i, d]
+                    else:
+                        inv = 1.0 / (s + SPAN / UNIT)
+                        square, weight = inv * inv, s * inv
+                    slope = (square - 4.0 * (weight * near)) * (near * near)
+                    parts[half].append(halves(pair_f[i, d] + (scale[i] * volume) * slope))
+            columns = [jnp.concatenate([x for pieces_of in half for x in pieces_of], axis=0)
+                       for half in parts]
+            lines = [jnp.concatenate(parts[0][i] + parts[1][i], axis=1) for i in range(together)]
+            return jnp.concatenate(columns, axis=1), jnp.concatenate(lines, axis=0)
+
+        def far_sums(p, factors, own_sum):
+            far_acc[p] = far_acc[p] + product(x_sums, factors[0])
+            return own_sum + product_turned(far_w[p], factors[1])
+
+        own_sum = over_far(devices // 2, far_factors, far_sums, jnp.concatenate(own_near, axis=1))
         for i, t in enumerate(members):
             total, moment = weighted(own_sum[:, i * LANES : (i + 1) * LANES])
             grad = win_c[window_place(t, SELF, cols), 0:3, :] * total - moment
@@ -459,12 +492,14 @@
 
     lax.fori_loop(0, tiles // together, group, 0)
 
-    def send_far(d, carry):
-        total, moment = weighted(far_acc[d])
-        send_ref[d, 0:3, :] = far_c[d, 0:3, :] * total - moment
+    def send_far(p, carry):
+        for half in range(2):
+            d = 2 * p + half
+            total, moment = weighted(far_acc[p, :, half * LANES : (half + 1) * LANES])
+            send_ref[d, 0:3, :] = far_c[d, 0:3, :] * total - moment
         return carry
 
-    lax.fori_loop(0, devices, send_far, 0)
+    lax.fori_loop(0, devices // 2, send_far, 0)
 
     def partner_grad(az, bs):
         place = (az + 1) * (cols + 2) + bs + 1
@@ -546,12 +581,13 @@
     dims = (rows, cols, dom_count, sub_count)
     devices = dom_count * sub_count
     tiles = rows * cols
-    assert width == LANES and tiles * CT == LANES and sub_count > 2
+    assert width == LANES and tiles * CT == LANES and sub_count > 2 and devices % 2 == 0
     slots = max(rows, cols)
     places = (rows + 2) * (cols + 2)
+    vec = (SUBLANES, LANES)
     together = 2 if devices <= 64 else 1
+    kept_shape = (together, devices, LANES, LANES) if devices <= 64 else (1, 1) + vec
     vmem = pltpu.MemorySpace.VMEM
-    vec = (SUBLANES, LANES)
 
     def call(body, ins, outs, scratch=(), room=8 << 20, space=vmem):
         return pl.pallas_call(
@@ -582,7 +618,7 @@
          bf16(tiles, LANES, KROWS), bf16(tiles, WROWS, 2 * LANES),
          bf16(places, KROWS, LANES), bf16(places, WROWS, 2 * LANES),
          f32(places, *vec), f32(places, *vec),
-         bf16(devices, KROWS, LANES), bf16(devices, WROWS, 2 * LANES),
+         bf16(devices // 2, KROWS, 2 * LANES), bf16(devices // 2, WROWS, 4 * LANES),
          f32(devices, *vec), f32(devices, tiles, LANES), f32(devices, tiles, LANES)],
         room=(8 << 20) + devices * (1 << 16))
     halo = exchanged(send)
@@ -593,9 +629,11 @@
          pltpu.VMEM((places,) + vec, jnp.float32),
          pltpu.VMEM((together, devices + NEAR, LANES, LANES), jnp.float32),
          pltpu.VMEM((together, devices + NEAR, LANES, LANES), jnp.float32),
-         pltpu.VMEM((devices, WROWS, LANES), jnp.float32),
+         pltpu.VMEM(kept_shape, jnp.float32),
+         pltpu.VMEM(kept_shape, jnp.float32),
+         pltpu.VMEM((devices // 2, WROWS, 2 * LANES), jnp.float32),
          pltpu.VMEM((places, WROWS, LANES), jnp.float32)],
-        room=(12 << 20) + together * devices * (3 << 16))
+        room=(13 << 20) + devices * (3 << 16 if together == 1 else 10 << 16))
     back = exchanged(send)
     shape = f32(rows, cols, LANES)
     forces, born_radii, radius_grad = call(

time: 62.8 us -> 62.4 us (level)
  no operation moved by 1% of the time
where the time goes in v5:
time: 62.4 us; the launch traced here: 62.1 us
  blocking collectives  36.3 us (58%)
  Pallas kernels  25.1 us (40%)
  between operations  0.7 us (1%)
    all_to_all x3, blocking collectives, exchanged(): return lax.all_to_all(blocks, AXES, 0, 0, tiled=True)  36.3 us
    pallas_call x4, Pallas kernels, call(): pl.pallas_call(lambda *refs: body(dims, *refs), out_shape=outs, in_specs=...  25.1 us

profile of v5, /device:TPU:0, one launch (start us, length us, event | category | flops | bytes accessed | tf_op | source)
XLA Modules:
  0.0 62.1 jit_solution(3103292512423323494)
XLA Ops:
  0.6 1.2 %pack_body.1 = (f32[16,24,128]{2,1,0:T(8,128)S(1)}, f32[8,128]{1,0:T(8,128)S(1)}, bf16[128,1024]{1,0:T(8,128)(2,1)S(1)}) custom-call(f32[3,2,4,128]{3,2,1,0:T(4,128)} %refs_2_.3, f32[2,4,128]{2,1,0:T(4,128)} %refs_3_.5, f32[2,4,128]{2,1,0:T(4,128)} %refs_4_.3, s32[2,4,128]{2,1,0:T(4,128)} %refs_3_.3), custom_call_target="tpu_custom_call" | custom-call | tf_op jit(solution)/shard_map/pack_body/pallas_call | solution.py:593
  1.8 0.0 copy-start
  1.8 0.0 copy-start.1
  1.8 0.0 copy-start.2
  1.8 0.0 copy-start.3
  1.8 16.3 %all_to_all.15.refs_1_ = f32[16,24,128]{2,1,0:T(8,128)S(1)} all-to-all(f32[16,24,128]{2,1,0:T(8,128)S(1)} %get-tuple-element.25), channel_id=1, replica_groups=mesh['groups'=2,'dom'=4,'sub'=4] {'dom','sub'}, dimensions={0} | all-to-all | bytes 393216 | tf_op jit(solution)/shard_map/all_to_all | solution.py:605
  18.1 0.0 copy-done
  18.1 0.0 copy-done.1
  18.1 0.0 copy-done.2
  18.1 0.0 copy-done.3
  18.2 4.9 %screen_body.1 = (f32[16,8,128]{2,1,0:T(8,128)S(1)}, f32[2,4,128]{2,1,0:T(4,128)S(1)}, bf16[8,128,48]{2,1,0:T(8,128)(2,1)S(1)}, bf16[8,16,256]{2,1,0:T(8,128)(2,...) custom-call(s32[2,4,8]{2,1,0:T(4,128)S(1)} %copy-done.3, ...), custom_call_target="tpu_custom_call" | custom-call | tf_op jit(solution)/shard_map/screen_body/pallas_call | solution.py:593
  23.0 9.5 %all_to_all.16.refs_2_ = f32[16,8,128]{2,1,0:T(8,128)S(1)} all-to-all(f32[16,8,128]{2,1,0:T(8,128)S(1)} %get-tuple-element.26), channel_id=1, replica_groups=mesh['groups'=2,'dom'=4,'sub'=4] {'dom','sub'}, dimensions={0} | all-to-all | bytes 131072 | tf_op jit(solution)/shard_map/all_to_all | solution.py:605
  32.5 18.1 %energy_body.1 = (f32[2,4,128]{2,1,0:T(4,128)S(1)}, f32[3,2,4,128]{3,2,1,0:T(4,128)S(1)}, f32[16,16,128]{2,1,0:T(8,128)S(1)}) custom-call(s32[2,4,8]{2,1,0:T(4,128)S(1)} %copy-done.3, f32[16,24,128]{2,1,0:T(8,128)S(1)} %all_to_all.15.refs_1_, f32[16,8,128]{2,1,0:T(8,128)S(1)} %all_to_all.16.refs_2_, f32[2,4,128]{2,1,0:T(4,128)S(1)} %copy-done.1, ...), custom_call_target="tpu_custom_call" | custom-call | tf_op jit(solution)/shard_map/energy_body/pallas_call | solution.py:593
  50.7 10.5 %all_to_all.17.refs_0_ = f32[16,16,128]{2,1,0:T(8,128)S(1)} all-to-all(f32[16,16,128]{2,1,0:T(8,128)S(1)} %get-tuple-element.39), channel_id=1, replica_groups=mesh['groups'=2,'dom'=4,'sub'=4] {'dom','sub'}, dimensions={0} | all-to-all | bytes 262144 | tf_op jit(solution)/shard_map/all_to_all | solution.py:605
  61.2 0.9 %finish_body.1 = (f32[3,2,4,128]{3,2,1,0:T(4,128)}, f32[2,4,128]{2,1,0:T(4,128)}, f32[2,4,128]{2,1,0:T(4,128)}) custom-call(f32[16,16,128]{2,1,0:T(8,128)S(1)} %all_to_all.17.refs_0_, f32[3,2,4,128]{3,2,1,0:T(4,128)S(1)} %get-tuple-element.40.refs_1_, f32[8,128]{1,0:T(8,128)S(1)} %get-tuple-element.41.refs_2_, ...), custom_call_target="tpu_custom_call" | custom-call | tf_op jit(solution)/shard_map/finish_body/pallas_call | solution.py:593
Async XLA Ops:
  1.8 16.3 %copy-start = (f32[3,2,4,128]{3,2,1,0:T(4,128)S(1)}, f32[3,2,4,128]{3,2,1,0:T(4,128)}, u32[]{:S(2)}) copy-start(f32[3,2,4,128]{3,2,1,0:T(4,128)} %refs_2_.3) | copy-start | bytes 36868
  1.8 16.3 %copy-start.1 = (f32[2,4,128]{2,1,0:T(4,128)S(1)}, f32[2,4,128]{2,1,0:T(4,128)}, u32[]{:S(2)}) copy-start(f32[2,4,128]{2,1,0:T(4,128)} %refs_3_.5) | copy-start | bytes 12292
  1.8 16.3 %copy-start.2 = (f32[2,4,128]{2,1,0:T(4,128)S(1)}, f32[2,4,128]{2,1,0:T(4,128)}, u32[]{:S(2)}) copy-start(f32[2,4,128]{2,1,0:T(4,128)} %refs_4_.3) | copy-start | bytes 12292
  1.8 16.3 %copy-start.3 = (s32[2,4,8]{2,1,0:T(4,128)S(1)}, s32[2,4,8]{2,1,0:T(4,128)}, u32[]{:S(2)}) copy-start(s32[2,4,8]{2,1,0:T(4,128)} %refs_0_.5) | copy-start | bytes 772

commit v6 on v5

--- a/solution.py
+++ b/solution.py
@@ -9,7 +9,7 @@
 LANES = 128
 SUBLANES = 8
 UNIT = 128.0
-TOGETHER = 4
+TOGETHER = 8
 KROWS = 48
 WROWS = 16
 SPAN = 64.0
@@ -343,10 +343,11 @@
 def energy_body(dims, near_ref, recv_ref, halo_ref, q_ref, r_ref, born_ref,
                 own_k, own_w, win_k, win_w, win_c, win_r, far_k, far_w, far_c, far_vol, far_q,
                 rgrad_ref, grad_ref, send_ref,
-                turned_ref, win_e, pair_f, pair_s, pair_i, pair_w, far_acc, win_acc):
+                turned_ref, win_e, *refs):
     rows, cols, dom_count, sub_count = dims
-    together = pair_f.shape[0]
-    kept = pair_i.shape[1] == dom_count * sub_count
+    stores, (far_acc, win_acc) = (refs[0:4], refs[4:8]), refs[8:]
+    together = refs[0].shape[0]
+    kept = refs[2].shape[1] == dom_count * sub_count
     devices = dom_count * sub_count
     slots = max(rows, cols)
     tiles = rows * cols
@@ -376,7 +377,8 @@
             for c, row in enumerate([born_ref[a, at, :], q_ref[a, at, :], r_ref[a, at, :]]):
                 turned_ref[a * cols + b, c] = turned(row)
 
-    def group(n, carry):
+    def energy_steps(n, store):
+        pair_f, pair_s, pair_i, pair_w = store
         members = [n * together + i for i in range(together)]
         own_rows = [[turned_ref[t, c] for c in range(3)] for t in members]
         own_inv = [1.0 / rows_of[0] for rows_of in own_rows]
@@ -387,22 +389,22 @@
             r = lax.rsqrt(s + (own_born * other_born) * e)
             return charge * (own_q * r), (r * r) * (1.0 - 0.25 * e)
 
-        born_near = []
-        for i, t in enumerate(members):
-            x, total = own_k[t], zero
-            for k in range(NEAR):
+        def near_energy(k, born_near):
+            out = list(born_near)
+            for i, t in enumerate(members):
                 place = window_place(t, k, cols)
                 other_born, other_inv, charge = [win_e[place, c : c + 1, :] for c in range(3)]
                 charge = flagged(near_ref, t, k, cols, charge)
                 if k == SELF:
                     charge = jnp.where(own_pair(), 0.0, charge)
-                s = product(x, win_k[place])
+                s = product(own_k[t], win_k[place])
                 qr, slope = pair(i, s, other_born, other_inv, charge)
                 f = qr * slope
                 pair_f[i, devices + k] = f
                 pair_s[i, devices + k] = s
-                total = total + (qr - s * f)
-            born_near.append(total)
+                out[i] = out[i] + (qr - s * f)
+            return tuple(out)
+
         def far_square(p):
             return product(jnp.concatenate([own_k[t] for t in members], axis=0), far_k[p])
 
@@ -427,24 +429,30 @@
                     out[i] = out[i] + qr * (weight - s * falling)
             return tuple(out)
 
-        born_far = over_far(devices // 2, far_square, far_energy, tuple([zero] * together))
-        scale = []
-        for i, t in enumerate(members):
-            _, own_q, own_rho = own_rows[i]
-            part = own_inv[i] * (UNIT * (0.5 * born_far[i] + born_near[i]))
-            own_part = own_q * own_inv[i]
-            rg = jnp.sum(part, axis=1, keepdims=True) + 0.5 * (own_part * own_part)
-            scale.append(rg * (own_rho * own_rho) * (1.0 / UNIT ** 3))
-            rgrad_ref[t // cols, pl.ds(t % cols, 1), :] = rg.T[0:1]
-
-        def halves(f):
-            high = f.astype(jnp.bfloat16)
-            return high, (f - high.astype(jnp.float32)).astype(jnp.bfloat16)
-
-        own_near = []
-        for i, t in enumerate(members):
-            total = no_force
-            for k in range(NEAR):
+        def finish(born_near, born_far):
+            scale = []
+            for i, t in enumerate(members):
+                _, own_q, own_rho = own_rows[i]
+                part = own_inv[i] * (UNIT * (0.5 * born_far[i] + born_near[i]))
+                own_part = own_q * own_inv[i]
+                rg = jnp.sum(part, axis=1, keepdims=True) + 0.5 * (own_part * own_part)
+                scale.append(rg * (own_rho * own_rho) * (1.0 / UNIT ** 3))
+                rgrad_ref[t // cols, pl.ds(t % cols, 1), :] = rg.T[0:1]
+            return scale
+
+        return near_energy, far_square, far_energy, finish
+
+    def halves(f):
+        high = f.astype(jnp.bfloat16)
+        return high, (f - high.astype(jnp.float32)).astype(jnp.bfloat16)
+
+    def chain_steps(n, store, scale):
+        pair_f, pair_s, pair_i, pair_w = store
+        members = [n * together + i for i in range(together)]
+
+        def near_chain(k, own_near):
+            out = list(own_near)
+            for i, t in enumerate(members):
                 place = window_place(t, k, cols)
                 volume = flagged(near_ref, t, k, cols, 4.0 * win_r[place, 1:2, :])
                 inv = 1.0 / (pair_s[i, devices + k] + win_r[place, 0:1, :])
@@ -452,10 +460,12 @@
                 if k == SELF:
                     f = jnp.where(own_pair(), 0.0, f)
                 high, low = halves(f)
-                total = total + product_turned(win_w[place], jnp.concatenate([high, low], axis=1))
+                out[i] = out[i] + product_turned(
+                    win_w[place], jnp.concatenate([high, low], axis=1))
                 win_acc[place] = win_acc[place] + product(
                     own_w[t], jnp.concatenate([high, low], axis=0))
-            own_near.append(total)
+            return tuple(out)
+
         x_sums = jnp.concatenate([own_w[t] for t in members], axis=1)
 
         def far_factors(p):
@@ -482,15 +492,63 @@
             far_acc[p] = far_acc[p] + product(x_sums, factors[0])
             return own_sum + product_turned(far_w[p], factors[1])
 
-        own_sum = over_far(devices // 2, far_factors, far_sums, jnp.concatenate(own_near, axis=1))
-        for i, t in enumerate(members):
-            total, moment = weighted(own_sum[:, i * LANES : (i + 1) * LANES])
-            grad = win_c[window_place(t, SELF, cols), 0:3, :] * total - moment
-            for c in range(3):
-                grad_ref[c, t // cols, pl.ds(t % cols, 1), :] = grad[c : c + 1]
-        return carry
-
-    lax.fori_loop(0, tiles // together, group, 0)
+        def finish(own_sum):
+            for i, t in enumerate(members):
+                total, moment = weighted(own_sum[:, i * LANES : (i + 1) * LANES])
+                grad = win_c[window_place(t, SELF, cols), 0:3, :] * total - moment
+                for c in range(3):
+                    grad_ref[c, t // cols, pl.ds(t % cols, 1), :] = grad[c : c + 1]
+
+        return near_chain, far_factors, far_sums, finish
+
+    pairs = devices // 2
+
+    def energy_of(n, store):
+        near_energy, far_square, far_energy, finish = energy_steps(n, store)
+        born_near = tuple([zero] * together)
+        for k in range(NEAR):
+            born_near = near_energy(k, born_near)
+        return finish(born_near, over_far(pairs, far_square, far_energy, tuple([zero] * together)))
+
+    def chain_of(n, store, scale):
+        near_chain, far_factors, far_sums, finish = chain_steps(n, store, scale)
+        own_near = tuple([no_force] * together)
+        for k in range(NEAR):
+            own_near = near_chain(k, own_near)
+        finish(over_far(pairs, far_factors, far_sums, jnp.concatenate(own_near, axis=1)))
+
+    def both_of(n, store, last_store, scale):
+        near_energy, far_square, far_energy, finish = energy_steps(n, store)
+        near_chain, far_factors, far_sums, finish_chain = chain_steps(n - 1, last_store, scale)
+        born_near, own_near = tuple([zero] * together), tuple([no_force] * together)
+        for k in range(NEAR):
+            born_near = near_energy(k, born_near)
+            own_near = near_chain(k, own_near)
+
+        def begin(p):
+            return far_square(p), far_factors(p)
+
+        def end(p, begun, carry):
+            return far_energy(p, begun[0], carry[0]), far_sums(p, begun[1], carry[1])
+
+        born_far, own_sum = over_far(
+            pairs, begin, end, (tuple([zero] * together), jnp.concatenate(own_near, axis=1)))
+        finish_chain(own_sum)
+        return finish(born_near, born_far)
+
+    groups = tiles // together
+    if kept:
+        scale = energy_of(0, stores[0])
+        for n in range(1, groups):
+            scale = both_of(n, stores[n % 2], stores[(n - 1) % 2], scale)
+        chain_of(groups - 1, stores[(groups - 1) % 2], scale)
+    else:
+
+        def group(n, carry):
+            chain_of(n, stores[0], energy_of(n, stores[0]))
+            return carry
+
+        lax.fori_loop(0, groups, group, 0)
 
     def send_far(p, carry):
         for half in range(2):
@@ -587,6 +645,7 @@
     vec = (SUBLANES, LANES)
     together = 2 if devices <= 64 else 1
     kept_shape = (together, devices, LANES, LANES) if devices <= 64 else (1, 1) + vec
+    second_shape = (together, devices + NEAR, LANES, LANES) if devices <= 64 else (1, 1) + vec
     vmem = pltpu.MemorySpace.VMEM
 
     def call(body, ins, outs, scratch=(), room=8 << 20, space=vmem):
@@ -631,9 +690,13 @@
          pltpu.VMEM((together, devices + NEAR, LANES, LANES), jnp.float32),
          pltpu.VMEM(kept_shape, jnp.float32),
          pltpu.VMEM(kept_shape, jnp.float32),
+         pltpu.VMEM(second_shape, jnp.float32),
+         pltpu.VMEM(second_shape, jnp.float32),
+         pltpu.VMEM(kept_shape, jnp.float32),
+         pltpu.VMEM(kept_shape, jnp.float32),
          pltpu.VMEM((devices // 2, WROWS, 2 * LANES), jnp.float32),
          pltpu.VMEM((places, WROWS, LANES), jnp.float32)],
-        room=(13 << 20) + devices * (3 << 16 if together == 1 else 10 << 16))
+        room=(13 << 20) + devices * (3 << 16 if together == 1 else 20 << 16))
     back = exchanged(send)
     shape = f32(rows, cols, LANES)
     forces, born_radii, radius_grad = call(

time: 62.4 us -> 61 us (0.978)
  Pallas kernels: 25.1 us -> 23.7 us
    pallas_call x4, Pallas kernels: 25.1 us -> 23.7 us  [call(): pl.pallas_call(lambda *refs: body(dims, *refs), out_shape=outs, in_specs=...]
where the time goes in v6:
time: 61 us; the launch traced here: 60.7 us
  blocking collectives  36.3 us (60%)
  Pallas kernels  23.7 us (39%)
  between operations  0.7 us (1%)
    all_to_all x3, blocking collectives, exchanged(): return lax.all_to_all(blocks, AXES, 0, 0, tiled=True)  36.3 us
    pallas_call x4, Pallas kernels, call(): pl.pallas_call(lambda *refs: body(dims, *refs), out_shape=outs, in_specs=...  23.7 us

profile of v6, /device:TPU:0, one launch (start us, length us, event | category | flops | bytes accessed | tf_op | source)
XLA Modules:
  0.0 60.7 jit_solution(4215514437688744072)
XLA Ops:
  0.6 1.2 %pack_body.1 = (f32[16,24,128]{2,1,0:T(8,128)S(1)}, f32[8,128]{1,0:T(8,128)S(1)}, bf16[128,1024]{1,0:T(8,128)(2,1)S(1)}) custom-call(f32[3,2,4,128]{3,2,1,0:T(4,128)} %refs_2_.3, f32[2,4,128]{2,1,0:T(4,128)} %refs_3_.5, f32[2,4,128]{2,1,0:T(4,128)} %refs_4_.3, s32[2,4,128]{2,1,0:T(4,128)} %refs_3_.3), custom_call_target="tpu_custom_call" | custom-call | tf_op jit(solution)/shard_map/pack_body/pallas_call | solution.py:652
  1.8 0.0 copy-start
  1.8 0.0 copy-start.1
  1.8 0.0 copy-start.2
  1.8 0.0 copy-start.3
  1.8 16.3 %all_to_all.15.refs_1_ = f32[16,24,128]{2,1,0:T(8,128)S(1)} all-to-all(f32[16,24,128]{2,1,0:T(8,128)S(1)} %get-tuple-element.25), channel_id=1, replica_groups=mesh['groups'=2,'dom'=4,'sub'=4] {'dom','sub'}, dimensions={0} | all-to-all | bytes 393216 | tf_op jit(solution)/shard_map/all_to_all | solution.py:664
  18.1 0.0 copy-done
  18.1 0.0 copy-done.1
  18.1 0.0 copy-done.2
  18.1 0.0 copy-done.3
  18.2 4.6 %screen_body.1 = (f32[16,8,128]{2,1,0:T(8,128)S(1)}, f32[2,4,128]{2,1,0:T(4,128)S(1)}, bf16[8,128,48]{2,1,0:T(8,128)(2,1)S(1)}, bf16[8,16,256]{2,1,0:T(8,128)(2,...) custom-call(s32[2,4,8]{2,1,0:T(4,128)S(1)} %copy-done.3, ...), custom_call_target="tpu_custom_call" | custom-call | tf_op jit(solution)/shard_map/screen_body/pallas_call | solution.py:652
  22.7 9.5 %all_to_all.16.refs_2_ = f32[16,8,128]{2,1,0:T(8,128)S(1)} all-to-all(f32[16,8,128]{2,1,0:T(8,128)S(1)} %get-tuple-element.26), channel_id=1, replica_groups=mesh['groups'=2,'dom'=4,'sub'=4] {'dom','sub'}, dimensions={0} | all-to-all | bytes 131072 | tf_op jit(solution)/shard_map/all_to_all | solution.py:664
  32.2 17.1 %energy_body.1 = (f32[2,4,128]{2,1,0:T(4,128)S(1)}, f32[3,2,4,128]{3,2,1,0:T(4,128)S(1)}, f32[16,16,128]{2,1,0:T(8,128)S(1)}) custom-call(s32[2,4,8]{2,1,0:T(4,128)S(1)} %copy-done.3, f32[16,24,128]{2,1,0:T(8,128)S(1)} %all_to_all.15.refs_1_, f32[16,8,128]{2,1,0:T(8,128)S(1)} %all_to_all.16.refs_2_, f32[2,4,128]{2,1,0:T(4,128)S(1)} %copy-done.1, ...), custom_call_target="tpu_custom_call" | custom-call | tf_op jit(solution)/shard_map/energy_body/pallas_call | solution.py:652
  49.3 10.5 %all_to_all.17.refs_0_ = f32[16,16,128]{2,1,0:T(8,128)S(1)} all-to-all(f32[16,16,128]{2,1,0:T(8,128)S(1)} %get-tuple-element.39), channel_id=1, replica_groups=mesh['groups'=2,'dom'=4,'sub'=4] {'dom','sub'}, dimensions={0} | all-to-all | bytes 262144 | tf_op jit(solution)/shard_map/all_to_all | solution.py:664
  59.8 0.9 %finish_body.1 = (f32[3,2,4,128]{3,2,1,0:T(4,128)}, f32[2,4,128]{2,1,0:T(4,128)}, f32[2,4,128]{2,1,0:T(4,128)}) custom-call(f32[16,16,128]{2,1,0:T(8,128)S(1)} %all_to_all.17.refs_0_, f32[3,2,4,128]{3,2,1,0:T(4,128)S(1)} %get-tuple-element.40.refs_1_, f32[8,128]{1,0:T(8,128)S(1)} %get-tuple-element.41.refs_2_, ...), custom_call_target="tpu_custom_call" | custom-call | tf_op jit(solution)/shard_map/finish_body/pallas_call | solution.py:652
Async XLA Ops:
  1.8 16.3 %copy-start = (f32[3,2,4,128]{3,2,1,0:T(4,128)S(1)}, f32[3,2,4,128]{3,2,1,0:T(4,128)}, u32[]{:S(2)}) copy-start(f32[3,2,4,128]{3,2,1,0:T(4,128)} %refs_2_.3) | copy-start | bytes 36868
  1.8 16.3 %copy-start.1 = (f32[2,4,128]{2,1,0:T(4,128)S(1)}, f32[2,4,128]{2,1,0:T(4,128)}, u32[]{:S(2)}) copy-start(f32[2,4,128]{2,1,0:T(4,128)} %refs_3_.5) | copy-start | bytes 12292
  1.8 16.3 %copy-start.2 = (f32[2,4,128]{2,1,0:T(4,128)S(1)}, f32[2,4,128]{2,1,0:T(4,128)}, u32[]{:S(2)}) copy-start(f32[2,4,128]{2,1,0:T(4,128)} %refs_4_.3) | copy-start | bytes 12292
  1.8 16.3 %copy-start.3 = (s32[2,4,8]{2,1,0:T(4,128)S(1)}, s32[2,4,8]{2,1,0:T(4,128)}, u32[]{:S(2)}) copy-start(s32[2,4,8]{2,1,0:T(4,128)} %refs_0_.5) | copy-start | bytes 772

commit v7 on v6

--- a/solution.py
+++ b/solution.py
@@ -54,6 +54,10 @@
 
 def far_unroll(pairs):
     return 8 if pairs % 8 == 0 else 1
+
+
+def short_loop(trips, step, carry):
+    return lax.fori_loop(0, trips, step, carry, unroll=trips <= 16)
 
 
 def pieces(value):
@@ -157,7 +161,7 @@
         send_ref[d, 0:8, :] = table
         return carry
 
-    lax.fori_loop(0, dom_count * sub_count, put, 0)
+    short_loop(dom_count * sub_count, put, 0)
     for rz in (-1, 0, 1):
         for rs in (-1, 0, 1):
             where = device_at(rz, rs, dom_count, sub_count)
@@ -275,7 +279,7 @@
             far_w[p, :, 2 * half * LANES : 2 * (half + 1) * LANES] = weights
         return carry
 
-    lax.fori_loop(0, devices // 2, put, 0)
+    short_loop(devices // 2, put, 0)
     mask_rows(dims, near_ref, (far_vol, far_q))
     none = jnp.zeros((SUBLANES - 3, LANES), jnp.float32)
     for place in range((rows + 2) * (cols + 2)):
@@ -364,7 +368,7 @@
         far_acc[p] = jnp.zeros((WROWS, 2 * LANES), jnp.float32)
         return carry
 
-    lax.fori_loop(0, devices // 2, put, 0)
+    short_loop(devices // 2, put, 0)
     for place in range(places):
         born, charge = [window_source(dims, place, halo_ref, own, 0, c) for c in range(2)]
         win_e[place, 0:1, :] = born * (1.0 / UNIT)
@@ -557,7 +561,7 @@
             send_ref[d, 0:3, :] = far_c[d, 0:3, :] * total - moment
         return carry
 
-    lax.fori_loop(0, devices // 2, send_far, 0)
+    short_loop(devices // 2, send_far, 0)
 
     def partner_grad(az, bs):
         place = (az + 1) * (cols + 2) + bs + 1
@@ -594,8 +598,8 @@
     def add(d, total):
         return total + recv_ref[d, 0:3, :]
 
-    centre_grad = lax.fori_loop(
-        0, dom_count * sub_count, add, jnp.zeros((3, LANES), jnp.float32))
+    centre_grad = short_loop(
+        dom_count * sub_count, add, jnp.zeros((3, LANES), jnp.float32))
     per_member = centre_grad / members_ref[0:3, :]
     born_out[...] = born_ref[...]
     rgrad_out[...] = rgrad_ref[...]

time: 61 us -> 60.3 us (0.989)
  Pallas kernels: 23.7 us -> 23 us
    pallas_call x4, Pallas kernels: 23.7 us -> 23 us  [call(): pl.pallas_call(lambda *refs: body(dims, *refs), out_shape=outs, in_specs=...]
where the time goes in v7:
time: 60.3 us; the launch traced here: 60 us
  blocking collectives  36.3 us (60%)
  Pallas kernels  23 us (38%)
  between operations  0.7 us (1%)
    all_to_all x3, blocking collectives, exchanged(): return lax.all_to_all(blocks, AXES, 0, 0, tiled=True)  36.3 us
    pallas_call x4, Pallas kernels, call(): pl.pallas_call(lambda *refs: body(dims, *refs), out_shape=outs, in_specs=...  23 us

profile of v7, /device:TPU:0, one launch (start us, length us, event | category | flops | bytes accessed | tf_op | source)
XLA Modules:
  0.0 60.0 jit_solution(6376337645326300221)
XLA Ops:
  0.6 1.1 %pack_body.1 = (f32[16,24,128]{2,1,0:T(8,128)S(1)}, f32[8,128]{1,0:T(8,128)S(1)}, bf16[128,1024]{1,0:T(8,128)(2,1)S(1)}) custom-call(f32[3,2,4,128]{3,2,1,0:T(4,128)} %refs_2_.3, f32[2,4,128]{2,1,0:T(4,128)} %refs_3_.5, f32[2,4,128]{2,1,0:T(4,128)} %refs_4_.3, s32[2,4,128]{2,1,0:T(4,128)} %refs_3_.3), custom_call_target="tpu_custom_call" | custom-call | tf_op jit(solution)/shard_map/pack_body/pallas_call | solution.py:656
  1.7 0.0 copy-start
  1.7 0.0 copy-start.1
  1.7 0.0 copy-start.2
  1.7 0.0 copy-start.3
  1.7 16.3 %all_to_all.15.refs_1_ = f32[16,24,128]{2,1,0:T(8,128)S(1)} all-to-all(f32[16,24,128]{2,1,0:T(8,128)S(1)} %get-tuple-element.25), channel_id=1, replica_groups=mesh['groups'=2,'dom'=4,'sub'=4] {'dom','sub'}, dimensions={0} | all-to-all | bytes 393216 | tf_op jit(solution)/shard_map/all_to_all | solution.py:668
  18.0 0.0 copy-done
  18.0 0.0 copy-done.1
  18.0 0.0 copy-done.2
  18.0 0.0 copy-done.3
  18.1 4.3 %screen_body.1 = (f32[16,8,128]{2,1,0:T(8,128)S(1)}, f32[2,4,128]{2,1,0:T(4,128)S(1)}, bf16[8,128,48]{2,1,0:T(8,128)(2,1)S(1)}, bf16[8,16,256]{2,1,0:T(8,128)(2,...) custom-call(s32[2,4,8]{2,1,0:T(4,128)S(1)} %copy-done.3, ...), custom_call_target="tpu_custom_call" | custom-call | tf_op jit(solution)/shard_map/screen_body/pallas_call | solution.py:656
  22.3 9.5 %all_to_all.16.refs_2_ = f32[16,8,128]{2,1,0:T(8,128)S(1)} all-to-all(f32[16,8,128]{2,1,0:T(8,128)S(1)} %get-tuple-element.26), channel_id=1, replica_groups=mesh['groups'=2,'dom'=4,'sub'=4] {'dom','sub'}, dimensions={0} | all-to-all | bytes 131072 | tf_op jit(solution)/shard_map/all_to_all | solution.py:668
  31.8 16.8 %energy_body.1 = (f32[2,4,128]{2,1,0:T(4,128)S(1)}, f32[3,2,4,128]{3,2,1,0:T(4,128)S(1)}, f32[16,16,128]{2,1,0:T(8,128)S(1)}) custom-call(s32[2,4,8]{2,1,0:T(4,128)S(1)} %copy-done.3, f32[16,24,128]{2,1,0:T(8,128)S(1)} %all_to_all.15.refs_1_, f32[16,8,128]{2,1,0:T(8,128)S(1)} %all_to_all.16.refs_2_, f32[2,4,128]{2,1,0:T(4,128)S(1)} %copy-done.1, ...), custom_call_target="tpu_custom_call" | custom-call | tf_op jit(solution)/shard_map/energy_body/pallas_call | solution.py:656
  48.6 10.5 %all_to_all.17.refs_0_ = f32[16,16,128]{2,1,0:T(8,128)S(1)} all-to-all(f32[16,16,128]{2,1,0:T(8,128)S(1)} %get-tuple-element.39), channel_id=1, replica_groups=mesh['groups'=2,'dom'=4,'sub'=4] {'dom','sub'}, dimensions={0} | all-to-all | bytes 262144 | tf_op jit(solution)/shard_map/all_to_all | solution.py:668
  59.2 0.8 %finish_body.1 = (f32[3,2,4,128]{3,2,1,0:T(4,128)}, f32[2,4,128]{2,1,0:T(4,128)}, f32[2,4,128]{2,1,0:T(4,128)}) custom-call(f32[16,16,128]{2,1,0:T(8,128)S(1)} %all_to_all.17.refs_0_, f32[3,2,4,128]{3,2,1,0:T(4,128)S(1)} %get-tuple-element.40.refs_1_, f32[8,128]{1,0:T(8,128)S(1)} %get-tuple-element.41.refs_2_, ...), custom_call_target="tpu_custom_call" | custom-call | tf_op jit(solution)/shard_map/finish_body/pallas_call | solution.py:656
Async XLA Ops:
  1.7 16.3 %copy-start = (f32[3,2,4,128]{3,2,1,0:T(4,128)S(1)}, f32[3,2,4,128]{3,2,1,0:T(4,128)}, u32[]{:S(2)}) copy-start(f32[3,2,4,128]{3,2,1,0:T(4,128)} %refs_2_.3) | copy-start | bytes 36868
  1.7 16.3 %copy-start.1 = (f32[2,4,128]{2,1,0:T(4,128)S(1)}, f32[2,4,128]{2,1,0:T(4,128)}, u32[]{:S(2)}) copy-start(f32[2,4,128]{2,1,0:T(4,128)} %refs_3_.5) | copy-start | bytes 12292
  1.7 16.3 %copy-start.2 = (f32[2,4,128]{2,1,0:T(4,128)S(1)}, f32[2,4,128]{2,1,0:T(4,128)}, u32[]{:S(2)}) copy-start(f32[2,4,128]{2,1,0:T(4,128)} %refs_4_.3) | copy-start | bytes 12292
  1.7 16.3 %copy-start.3 = (s32[2,4,8]{2,1,0:T(4,128)S(1)}, s32[2,4,8]{2,1,0:T(4,128)}, u32[]{:S(2)}) copy-start(s32[2,4,8]{2,1,0:T(4,128)} %refs_0_.5) | copy-start | bytes 772
